TPU v7x, 32 devices: a whole 2x2x4 slice. The times are simulated.
32 devices in a mesh: blk: 32 (over z, y, x, core).
Axes of the slice: x: 2, y: 2, z: 4, core: 2. Of those that a mesh axis runs over, the one named last changes fastest.
Arguments:
- features: bfloat16 [128, 352, 2048], P('blk'), may hold values from -6 to 6
- weight: bfloat16 [2048, 2048], replicated, may hold values from -0.375 to 0.375
- bias: float32 [2048], replicated, may hold values from -3 to 3
- cotangent: bfloat16 [128, 352, 2048], P('blk'), may hold values from -6 to 6
- segment_ids: int32 [128, 352], P('blk'), may hold values from 0 to 7, never falling along the last dimension, each value on 1 to 88 neighbouring positions
- neighbour_offsets: int32 [128, 352, 64], P('blk'), may hold values from 0 to 4095
- neighbour_mask: int32 [128, 352, 64], P('blk'), may hold values 0 or 1
- halo_edges: int32 [128, 2, 352, 8], P('blk'), may hold values from 0 to 63
- halo_mask: int32 [128, 2, 352, 8], P('blk'), may hold values 0 or 1
- boundary_rows: int32 [128, 2, 64], P('blk'), may hold values from 0 to 351
Outputs:
- activations: bfloat16 [128, 352, 2048], P('blk')
- grad_features: bfloat16 [128, 352, 2048], P('blk')
- grad_weight: float32 [2048, 2048], replicated
- grad_bias: float32 [2048], replicated
Inputs may be any that keep to these rules, and one draw needn't show every extreme that they name: `segment_ids`: within a slot segment ids never fall; each of the 8 clusters has 1 to 88 rows and one has exactly 88.
All inputs are finite; a program needn't handle non-finite values. No bound on the sum of `neighbour_mask` or of `halo_mask` on one device may be relied on, other than what follows from the above.
Results may differ from a plain program's by a relative error of at most 0.011.
Values may be sent and summed in bfloat16 or wider, within the bound.
A program may use at most 192 MiB of HBM per device.

v0:
```python
import jax
import jax.numpy as jnp
from jax import lax
from jax.sharding import PartitionSpec as P

B = 64


def passed_along(value, axis, steps):
    count = lax.axis_size(axis)
    pairs = [(source, (source + steps) % count) for source in range(count)]
    return lax.ppermute(value, axis, pairs)


def tally(picks, marks, width):
    places = jnp.arange(width, dtype=jnp.int32)
    hot = picks[:, :, None] == places[None, None, :]
    return jnp.sum(jnp.where(hot, marks[:, :, None], 0), axis=1)


def slot_tables(items):
    seg, offsets, marks, edges, edge_marks = items
    rows = seg.shape[0]
    order = jnp.arange(rows, dtype=jnp.int32)
    same = seg[:, None] == seg[None, :]
    start = jnp.min(jnp.where(same, order[None, :], rows), axis=1)
    extent = jnp.sum(same.astype(jnp.int32), axis=1)
    picks = start[:, None] + offsets % extent[:, None]
    local = tally(picks, marks, rows) + 2 * (order[:, None] == order[None, :]).astype(jnp.int32)
    joined = jnp.concatenate([edges[0], edges[1] + B], axis=1)
    joined_marks = jnp.concatenate([edge_marks[0], edge_marks[1]], axis=1)
    halo = tally(joined, joined_marks, 2 * B)
    degree = (
        jnp.sum(marks, axis=1) + jnp.sum(edge_marks[0], axis=1) + jnp.sum(edge_marks[1], axis=1)
    )
    scale = 1.0 / (1.0 + degree.astype(jnp.float32))
    return (local.astype(jnp.bfloat16), halo.astype(jnp.bfloat16), scale)


def per_device(
    features,
    weight,
    bias,
    cotangent,
    segment_ids,
    neighbour_offsets,
    neighbour_mask,
    halo_edges,
    halo_mask,
    boundary_rows,
):
    slots, rows, width = features.shape
    rim = boundary_rows.shape[2]
    local_counts, halo_counts, scale = lax.map(
        slot_tables, (segment_ids, neighbour_offsets, neighbour_mask, halo_edges, halo_mask)
    )
    sent = jax.vmap(lambda block, picks: block[picks])(features, boundary_rows)
    from_prev = passed_along(sent[slots - 1, 1], "blk", 1)
    from_next = passed_along(sent[0, 0], "blk", -1)
    before = jnp.concatenate([from_prev[None], sent[: slots - 1, 1]], axis=0)
    after = jnp.concatenate([sent[1:, 0], from_next[None]], axis=0)
    received = jnp.concatenate([before, after], axis=1)
    summed = jnp.einsum("srk,skf->srf", local_counts, features, preferred_element_type=jnp.float32)
    summed = summed + jnp.einsum(
        "srk,skf->srf", halo_counts, received, preferred_element_type=jnp.float32
    )
    mixed = (scale[:, :, None] * summed).astype(jnp.bfloat16).reshape(slots * rows, width)
    pre = jnp.dot(mixed, weight, preferred_element_type=jnp.float32) + bias[None, :]
    sigma = jax.nn.sigmoid(pre)
    activations = (pre * sigma).astype(jnp.bfloat16)
    incoming = cotangent.reshape(slots * rows, width)
    grad_pre = (incoming.astype(jnp.float32) * (sigma * (1.0 + pre * (1.0 - sigma)))).astype(
        jnp.bfloat16
    )
    bias_term = jnp.sum(grad_pre, axis=0, dtype=jnp.float32)
    grad_mixed = lax.dot_general(
        grad_pre, weight, (((1,), (1,)), ((), ())), preferred_element_type=jnp.float32
    ).astype(jnp.bfloat16)
    grad_summed = (
        (scale.reshape(-1)[:, None] * grad_mixed.astype(jnp.float32))
        .astype(jnp.bfloat16)
        .reshape(slots, rows, width)
    )
    grad_local = jnp.einsum(
        "srk,srf->skf", local_counts, grad_summed, preferred_element_type=jnp.float32
    )
    grad_received = jnp.einsum(
        "srk,srf->skf", halo_counts, grad_summed, preferred_element_type=jnp.float32
    )
    toward_prev = grad_received[:, :rim]
    toward_next = grad_received[:, rim:]
    back_prev = passed_along(toward_next[slots - 1].astype(jnp.bfloat16), "blk", 1).astype(
        jnp.float32
    )
    back_next = passed_along(toward_prev[0].astype(jnp.bfloat16), "blk", -1).astype(jnp.float32)
    grad_first = jnp.concatenate([back_prev[None], toward_next[: slots - 1]], axis=0)
    grad_second = jnp.concatenate([toward_prev[1:], back_next[None]], axis=0)
    grad_sent = jnp.stack([grad_first, grad_second], axis=1)
    grad_features = jax.vmap(
        lambda block, picks, values: block.at[picks.reshape(-1)].add(
            values.reshape(-1, values.shape[-1])
        )
    )(grad_local, boundary_rows, grad_sent)
    weight_term = lax.dot_general(
        mixed, grad_pre, (((0,), (0,)), ((), ())), preferred_element_type=jnp.float32
    )
    grad_weight, grad_bias = lax.psum((weight_term, bias_term), "blk")
    return (
        activations.reshape(slots, rows, width),
        grad_features.astype(jnp.bfloat16),
        grad_weight,
        grad_bias,
    )


def solution(mesh):
    in_specs = (
        P("blk", None, None),
        P(),
        P(),
        P("blk", None, None),
        P("blk", None),
        P("blk", None, None),
        P("blk", None, None),
        P("blk", None, None, None),
        P("blk", None, None, None),
        P("blk", None, None),
    )
    out_specs = (P("blk", None, None), P("blk", None, None), P(), P())
    return jax.shard_map(
        per_device, mesh=mesh, in_specs=in_specs, out_specs=out_specs, check_vma=False
    )
```

profile of v0, /device:TPU:0, one launch (start us, length us, event | category | flops | bytes accessed | tf_op | source)
XLA Modules:
  0.0 450.7 jit_solution(13690859779666592961)
XLA Ops:
  8.0 10.0 %gather_fusion = bf16[512,2048]{1,0:T(8,128)(2,1)S(1)} fusion(bf16[4,352,2048]{2,1,0:T(8,128)(2,1)} %param.12, s32[512]{0:T(512)S(1)} %reshape.233), kind=kCustom, calls=%fused_computation | custom fusion | bytes 4198400 | tf_op jit(solution)/shard_map/vmap()/gather | solution.py:57
  19.2 5.9 %collective-permute-start.1 = (bf16[64,2048]{1,0:T(8,128)(2,1)}, bf16[64,2048]{1,0:T(8,128)(2,1)}, u32[]{:S(2)}, u32[]{:S(2)}) collective-permute-start(bf16[64,2048]{1,0:T(8,128)(2,1)} %get-tuple-element.101), channel_id=1, source_target_pairs={{0,31},{1,0},{2,1},{3,2},{4,3},{5,4},{6,5},{7,6},{8,7},{9,8},{10,9... | collective-permute-start | bytes 786440 | tf_op jit(solution)/shard_map/ppermute | solution.py:12
  25.2 76.0 %while.14 = (s32[]{:T(128)}, bf16[4,352,352]{2,1,0:T(8,128)(2,1)}, bf16[4,352,128]{2,1,0:T(8,128)(2,1)}, f32[4,352]{1,0:T(4,128)S(1)}, s32[4,352]{1,0:T(4,128)},...) while((s32[]{:T(128)}, bf16[4,352,352]{2,1,0:T(8,128)(2,1)}, ...), condition=%wide.region_8.9_spmd, body=%wide.region_0.8_spmd.sunk | while | flops 27167712 | bytes 2960097 | solution.py:54
  29.3 9.3 %select_reduce_fusion.4 = s32[352,352]{1,0:T(8,128)S(1)} fusion(s32[352,64]{1,0:T(8,128)S(1)} %copy.47, s32[352,64]{1,0:T(8,128)S(1)} %copy.48), kind=kLoop, calls=%fused_computation.2.clone.1 | loop fusion | flops 23665664 | bytes 675840 | tf_op jit(solution)/shard_map/while/body/eval_jaxpr/reduce_sum | solution.py:18
  41.1 2.3 select_reduce_fusion.5
  48.3 9.3 %select_reduce_fusion.4 = s32[352,352]{1,0:T(8,128)S(1)} fusion(s32[352,64]{1,0:T(8,128)S(1)} %copy.47, s32[352,64]{1,0:T(8,128)S(1)} %copy.48), kind=kLoop, calls=%fused_computation.2.clone.1 | loop fusion | flops 23665664 | bytes 675840 | tf_op jit(solution)/shard_map/while/body/eval_jaxpr/reduce_sum | solution.py:18
  60.1 2.3 select_reduce_fusion.5
  67.2 9.3 %select_reduce_fusion.4 = s32[352,352]{1,0:T(8,128)S(1)} fusion(s32[352,64]{1,0:T(8,128)S(1)} %copy.47, s32[352,64]{1,0:T(8,128)S(1)} %copy.48), kind=kLoop, calls=%fused_computation.2.clone.1 | loop fusion | flops 23665664 | bytes 675840 | tf_op jit(solution)/shard_map/while/body/eval_jaxpr/reduce_sum | solution.py:18
  79.1 2.3 select_reduce_fusion.5
  86.2 9.3 %select_reduce_fusion.4 = s32[352,352]{1,0:T(8,128)S(1)} fusion(s32[352,64]{1,0:T(8,128)S(1)} %copy.47, s32[352,64]{1,0:T(8,128)S(1)} %copy.48), kind=kLoop, calls=%fused_computation.2.clone.1 | loop fusion | flops 23665664 | bytes 675840 | tf_op jit(solution)/shard_map/while/body/eval_jaxpr/reduce_sum | solution.py:18
  98.1 2.3 select_reduce_fusion.5
  101.1 5.5 %fusion.28 = f32[4,352,2048]{2,1,0:T(8,128)S(1)} fusion(bf16[4,352,352]{2,1,0:T(8,128)(2,1)} %get-tuple-element.54, bf16[4,352,2048]{2,1,0:T(8,128)(2,1)} %param.12), kind=kOutput, calls=%fused_computation.78 | convolution fusion | flops 2030043136 | bytes 18292736 | tf_op jit(solution)/shard_map/srk,skf->srf/dot_general | solution.py:63
  107.7 3.0 multiply_convert_fusion.2
  110.8 21.8 %convert_reduce_fusion = (f32[2048]{0:T(1024)S(1)}, bf16[1408,2048]{1,0:T(8,128)(2,1)S(1)}, bf16[1408,2048]{1,0:T(8,128)(2,1)}) fusion(f32[2048]{0:T(1024)S(1)} %copy-done.3, bf16[4,352,2048]{2,1,0:T(8,128)(2,1)} %param.15, bf16[1408,2048]{1,0:T(8,128)(2,1)S(1)} %bitcast.89, bf16[2048,2048]{1,0:T(8,128)(2,1)} %param.13), kind=kOutput, calls=%fused_computation.36 | convolution fusion | flops 11854411776 | bytes 31473664 | tf_op jit(solution)/shard_map/dot_general | solution.py:68
  132.6 2.5 copy-done.4
  135.2 16.5 %fusion.30 = f32[2048,2048]{1,0:T(8,128)} fusion(bf16[1408,2048]{1,0:T(8,128)(2,1)S(1)} %bitcast.90, bf16[1408,2048]{1,0:T(8,128)(2,1)S(1)} %get-tuple-element.88), kind=kOutput, calls=%fused_computation.80 | convolution fusion | flops 11811160064 | bytes 28311552 | tf_op jit(solution)/shard_map/dot_general | solution.py:104
  152.4 17.7 %multiply_convert_fusion = bf16[1408,2048]{1,0:T(8,128)(2,1)S(1)} fusion(bf16[1408,2048]{1,0:T(8,128)(2,1)} %copy-done.4, bf16[2048,2048]{1,0:T(8,128)(2,1)} %param.13, f32[1408]{0:T(1024)S(1)} %mul.36), kind=kOutput, calls=%fused_computation.37 | convolution fusion | flops 11822694400 | bytes 19928576 | tf_op jit(solution)/shard_map/dot_general | solution.py:76
  172.3 6.2 %fusion.29 = f32[4,352,2048]{2,1,0:T(8,128)} fusion(bf16[4,352,352]{2,1,0:T(8,128)(2,1)S(1)} %copy-done, bf16[4,352,2048]{2,1,0:T(8,128)(2,1)S(1)} %bitcast.85), kind=kOutput, calls=%fused_computation.79 | convolution fusion | flops 2030043136 | bytes 18292736 | tf_op jit(solution)/shard_map/srk,srf->skf/dot_general | solution.py:84
  178.6 5.3 %collective-permute-start.3 = (bf16[64,2048]{1,0:T(8,128)(2,1)}, bf16[64,2048]{1,0:T(8,128)(2,1)}, u32[]{:S(2)}, u32[]{:S(2)}) collective-permute-start(bf16[64,2048]{1,0:T(8,128)(2,1)} %get-tuple-element.99), channel_id=1, source_target_pairs={{0,31},{1,0},{2,1},{3,2},{4,3},{5,4},{6,5},{7,6},{8,7},{9,8},{10,9... | collective-permute-start | bytes 786440 | tf_op jit(solution)/shard_map/ppermute | solution.py:12
  184.0 38.6 %psum.15 = f32[2048]{0:T(1024)} all-reduce(f32[2048]{0:T(1024)S(1)} %get-tuple-element.87), channel_id=1, replica_groups=mesh['blk'=32] {'blk'}, use_global_device_ids=true, to_apply=%region_12.13 | all-reduce | flops 2048 | bytes 16384 | tf_op jit(solution)/shard_map/psum | solution.py:107
  226.8 98.9 %scatter_fusion = f32[4,352,2048]{2,1,0:T(8,128)} fusion(f32[4,352,2048]{2,1,0:T(8,128)} %fusion.29, s32[512]{0:T(512)S(1)} %fusion.22, f32[512,2048]{1,0:T(8,128)} %bitcast.86), kind=kCustom, calls=%fused_computation.1 | custom fusion | flops 1048576 | bytes 12587008 | tf_op jit(solution)/shard_map/vmap()/scatter-add | solution.py:100
  325.7 7.7 %convert_element_type.88 = bf16[4,352,2048]{2,1,0:T(8,128)(2,1)} convert(f32[4,352,2048]{2,1,0:T(8,128)} %scatter_fusion) | non-fusion elementwise | flops 2883584 | bytes 17301504 | tf_op jit(solution)/shard_map/convert_element_type | solution.py:110
  333.5 98.6 %all-reduce.2.cloned.1.call-done = f32[2048,2048]{1,0:T(8,128)} async-done(((f32[2048,2048]{1,0:T(8,128)}), f32[2048,2048]{1,0:T(8,128)}) %all-reduce.2.cloned.1.call-update) | async-done | bytes 16777232 | tf_op jit(solution)/shard_map/psum | solution.py:107
  432.0 11.8 %copy.68 = f32[2048,2048]{1,0:T(8,128)} copy(f32[2048,2048]{1,0:T(8,128)} %all-reduce.2.cloned.1.call-done) | data formatting | bytes 33554432
  (112 shorter events, 39.5 us)
Async XLA Ops:
  7.2 424.9 %all-reduce.2.cloned.1.call-start = ((), (), s32[]{:S(2)}) async-start(), calls=%async_computation | async-start | bytes 33554432 | tf_op jit(solution)/shard_map/psum | solution.py:107
  18.8 88.9 %collective-permute-start = (bf16[64,2048]{1,0:T(8,128)(2,1)}, bf16[64,2048]{1,0:T(8,128)(2,1)}, u32[]{:S(2)}, u32[]{:S(2)}) collective-permute-start(bf16[64,2048]{1,0:T(8,128)(2,1)} %get-tuple-element.100), channel_id=1, source_target_pairs={{0,1},{1,2},{2,3},{3,4},{4,5},{5,6},{6,7},{7,8},{8,9},{9,10},{10,1... | collective-permute-start | bytes 786440 | tf_op jit(solution)/shard_map/ppermute | solution.py:12
  19.2 88.5 %collective-permute-start.1 = (bf16[64,2048]{1,0:T(8,128)(2,1)}, bf16[64,2048]{1,0:T(8,128)(2,1)}, u32[]{:S(2)}, u32[]{:S(2)}) collective-permute-start(bf16[64,2048]{1,0:T(8,128)(2,1)} %get-tuple-element.101), channel_id=1, source_target_pairs={{0,31},{1,0},{2,1},{3,2},{4,3},{5,4},{6,5},{7,6},{8,7},{9,8},{10,9... | collective-permute-start | bytes 786440 | tf_op jit(solution)/shard_map/ppermute | solution.py:12
  101.1 6.6 %copy-start.1 = (bf16[4,352,128]{2,1,0:T(8,128)(2,1)S(1)}, bf16[4,352,128]{2,1,0:T(8,128)(2,1)}, u32[]{:S(2)}) copy-start(bf16[4,352,128]{2,1,0:T(8,128)(2,1)} %get-tuple-element.55) | copy-start | bytes 1081348
  107.7 3.1 copy-start.3
  132.6 2.5 copy-start.4
  151.6 0.7 copy-start.2
  170.1 2.2 copy-start
  172.3 50.3 %collective-permute-start.2 = (bf16[64,2048]{1,0:T(8,128)(2,1)}, bf16[64,2048]{1,0:T(8,128)(2,1)S(1)}, u32[]{:S(2)}, u32[]{:S(2)}) collective-permute-start(bf16[64,2048]{1,0:T(8,128)(2,1)} %get-tuple-element.98), channel_id=1, source_target_pairs={{0,1},{1,2},{2,3},{3,4},{4,5},{5,6},{6,7},{7,8},{8,9},{9,10},{10,1... | collective-permute-start | bytes 786440 | tf_op jit(solution)/shard_map/ppermute | solution.py:12
  178.6 44.2 %collective-permute-start.3 = (bf16[64,2048]{1,0:T(8,128)(2,1)}, bf16[64,2048]{1,0:T(8,128)(2,1)}, u32[]{:S(2)}, u32[]{:S(2)}) collective-permute-start(bf16[64,2048]{1,0:T(8,128)(2,1)} %get-tuple-element.99), channel_id=1, source_target_pairs={{0,31},{1,0},{2,1},{3,2},{4,3},{5,4},{6,5},{7,6},{8,7},{9,8},{10,9... | collective-permute-start | bytes 786440 | tf_op jit(solution)/shard_map/ppermute | solution.py:12
Sparse Core Ops, SparseCore 0:
  151.8 280.2 all-reduce.1
where the time goes:
time: 453 us; the launch traced here: 451 us
  other arithmetic  180 us (40%)
  waiting for transfers between devices  98.6 us (22%)
  matrix products  72.1 us (16%)
  blocking collectives  38.6 us (9%)
  local copies, waits for them, and re-layouts  35.2 us (8%)
  between operations  14.2 us (3%)
  starting transfers between devices  11.7 us (3%)
    scatter-add x2, other arithmetic, per_device(): block.at[picks.reshape(-1)].add(values.reshape(-1, values.shape[-1]))  98.9 us
    psum x1, waiting for transfers between devices, per_device(): grad_weight, grad_bias = lax.psum((weight_term, bias_term), 'blk')  98.6 us
    reduce_sum x8, other arithmetic, tally(): return jnp.sum(jnp.where(hot, marks[:, :, None], 0), axis=1)  46.6 us
    psum x1, blocking collectives, per_device(): grad_weight, grad_bias = lax.psum((weight_term, bias_term), 'blk')  38.6 us
    dot_general x1, matrix products, per_device(): jnp.dot(mixed, weight, preferred_element_type=jnp.float32) + bias[None, :]  21.8 us
    dot_general x1, matrix products, per_device(): lax.dot_general(grad_pre, weight, (((1,), (1,)), ((), ())), preferred_ele...  17.7 us
    dot_general x1, matrix products, per_device(): lax.dot_general(mixed, grad_pre, (((0,), (0,)), ((), ())), preferred_elem...  16.5 us
    unnamed x11, local copies, waits for them, and re-layouts  14.9 us
  transfers between devices with their start and end apart: 5, of which 1 were waited for; matrix products, arithmetic and copies ran while one was open for 49% of the time, Pallas kernels for 0%

commit v1 on v0

v1 whole, which is shorter than its diff:
```python
import functools

import jax
import jax.numpy as jnp
from jax import lax
from jax.experimental import pallas as pl
from jax.experimental.pallas import tpu as pltpu
from jax.sharding import PartitionSpec as P

bf16 = jnp.bfloat16
f32 = jnp.float32
MESH = pl.DeviceIdType.MESH
CH = 256
H = 128


def neighbours(me):
    core = me % 2
    bits = [core, (me // 2) % 2, (me // 4) % 2, (me // 8) % 2, me // 16]
    return bits, [me + (1 << i) - (2 << i) * b for i, b in enumerate(bits)]


def main_kernel(
    mixed, w, bias, cot,
    act, gp, ag, gb,
    mixed_v, w_v, bias_v, cot_v, act_v, gp_v, pre_v,
    snd, rc, acc, rf, ra, rs, rb, gb_v, gr,
    lsem, wsem, csem, asem, gsem, ksem, ssem, rsem, bsem, brsem,
):
    me = lax.axis_index("blk")
    rows, width = mixed_v.shape
    nch = width // CH
    half = width // 2
    quart = half // 2
    (core, bx, by, bz1, bz2), (pc, px, py, pz1, pz2) = neighbours(me)
    first = [px * (1 - core) + py * core, py * (1 - core) + px * core]
    fbit = [bx * (1 - core) + by * core, by * (1 - core) + bx * core]
    second = [first[1], first[0]]
    sbit = [fbit[1], fbit[0]]

    barrier = pltpu.get_barrier_semaphore()
    for p in (pc, px, py, pz1, pz2):
        pl.semaphore_signal(barrier, inc=1, device_id=(p,), device_id_type=MESH)

    def local(src, dst, sem):
        return pltpu.make_async_copy(src, dst, sem)

    def w_in(k):
        c = pl.multiple_of(k * CH, CH)
        return local(w.at[:, pl.ds(c, CH)], w_v.at[:, pl.ds(c, CH)], wsem.at[k])

    def cot_in(k):
        c = pl.multiple_of(k * CH, CH)
        return local(cot.at[:, pl.ds(c, CH)], cot_v.at[k % 2], csem.at[k % 2])

    def act_out(k):
        c = pl.multiple_of(k * CH, CH)
        return local(act_v.at[k % 2], act.at[:, pl.ds(c, CH)], asem.at[k % 2])

    local(mixed, mixed_v, lsem.at[0]).start()
    local(bias, bias_v, lsem.at[1]).start()
    w_in(0).start()
    cot_in(0).start()
    for k in range(1, nch):
        w_in(k).start()
    local(mixed, mixed_v, lsem.at[0]).wait()
    local(bias, bias_v, lsem.at[1]).wait()
    pl.semaphore_wait(barrier, 5)

    def remote(src, dst, k, s, to):
        return pltpu.make_async_remote_copy(
            src, dst, ssem.at[k, s], rsem.at[k, s], device_id=(to,), device_id_type=MESH
        )

    def rf_rows(i):
        return pl.multiple_of(quart * i, 64)

    def at(i, level, flip):
        r = quart * i
        size = quart
        picks = [bz1, sbit[i], bz2]
        for j in range(level):
            size = size // 2
            b = picks[j]
            if flip and j == level - 1:
                b = 1 - b
            r = r + size * b
        return pl.ds(pl.multiple_of(r, 64), size)

    def core_rs(k):
        return remote(snd.at[k], rc.at[k], k, 0, pc)

    def f_rs(k, i):
        return remote(acc.at[k, 1 - fbit[i], at(i, 0, False)], rf.at[k, i], k, 1 + i, first[i])

    def a_rs(k, i):
        return remote(acc.at[k, fbit[i], at(i, 1, True)], ra.at[k, i], k, 3 + i, pz1)

    def s_rs(k, i):
        return remote(acc.at[k, fbit[i], at(i, 2, True)], rs.at[k, i], k, 5 + i, second[i])

    def b_rs(k, i):
        return remote(acc.at[k, fbit[i], at(i, 3, True)], rb.at[k, i], k, 7 + i, pz2)

    def ag_at(k, i, level):
        d = at(i, level, False)
        return ag.at[2 * k + fbit[i], pl.ds(pl.multiple_of(half * core + d.start, 64), d.size)]

    def keep(k, i):
        return local(acc.at[k, fbit[i], at(i, 3, False)], ag_at(k, i, 3), ksem.at[k, i])

    def b_ag(k, i):
        return remote(acc.at[k, fbit[i], at(i, 3, False)], ag_at(k, i, 3), k, 9 + i, pz2)

    def s_ag(k, i):
        return remote(ag_at(k, i, 2), ag_at(k, i, 2), k, 11 + i, second[i])

    def a_ag(k, i):
        return remote(ag_at(k, i, 1), ag_at(k, i, 1), k, 13 + i, pz1)

    def f_ag(k, i):
        return remote(ag_at(k, i, 0), ag_at(k, i, 0), k, 15 + i, first[i])

    def c_ag(k, j):
        part = ag.at[2 * k + j, pl.ds(pl.multiple_of(half * core, 64), half)]
        return remote(part, part, k, 17 + j, pc)

    def when(t, s, f):
        k = t - s

        @pl.when((k >= 0) & (k < nch))
        def _():
            f(k)

    def s1(k):
        core_rs(k).wait_recv()
        for j in range(2):
            acc[k, j] = acc[k, j] + rc[k, j]
        for i in range(2):
            f_rs(k, i).start()

    def fold(wait, level, buf, nxt):
        def run(k):
            for i in range(2):
                wait(k, i).wait_recv()
                d = at(i, level, False)
                acc[k, fbit[i], d] = acc[k, fbit[i], d] + buf[k, i]
                nxt(k, i)

        return run

    def final(k, i):
        keep(k, i).start()
        b_ag(k, i).start()

    def s6(k):
        for i in range(2):
            keep(k, i).wait()
            b_ag(k, i).wait_recv()
            s_ag(k, i).start()

    def s7(k):
        for i in range(2):
            s_ag(k, i).wait_recv()
            a_ag(k, i).start()

    def s8(k):
        for i in range(2):
            a_ag(k, i).wait_recv()
            f_ag(k, i).start()

    def s9(k):
        for i in range(2):
            f_ag(k, i).wait_recv()
        for j in range(2):
            c_ag(k, j).start()

    def s10(k):
        for j in range(2):
            c_ag(k, j).wait_recv()

    def compute(k):
        c = pl.multiple_of(k * CH, CH)
        w_in(k).wait()
        cot_in(k).wait()

        @pl.when(k + 1 < nch)
        def _():
            cot_in(k + 1).start()

        @pl.when(k >= 2)
        def _():
            act_out(k - 2).wait()

        b = bias_v[pl.ds(k, 1), :]
        mt = rows // 2
        sums = jnp.zeros((1, CH), f32)
        for m in range(2):
            d = pl.ds(m * mt, mt)
            pre = jnp.dot(mixed_v[d, :], w_v[:, pl.ds(c, CH)], preferred_element_type=f32) + b
            sig = 0.5 * jnp.tanh(0.5 * pre) + 0.5
            out = pre * sig
            act_v[k % 2, d, :] = out.astype(bf16)
            g = (cot_v[k % 2, d, :].astype(f32) * (sig + out * (1.0 - sig))).astype(bf16)
            gp_v[d, pl.ds(c, CH)] = g
            sums = sums + jnp.sum(g.astype(f32), axis=0, keepdims=True)
        gb_v[0, pl.ds(k, 1), :] = sums
        act_out(k).start()
        local(gp_v.at[:, pl.ds(c, CH)], gp.at[:, pl.ds(c, CH)], gsem.at[k]).start()
        dims = (((0,), (0,)), ((), ()))
        g = gp_v[:, pl.ds(c, CH)]
        there = pl.multiple_of(half * (1 - core), half)
        part = lax.dot_general(mixed_v[:, pl.ds(there, half)], g, dims, preferred_element_type=f32)
        snd[k, 0] = part[:, :H].astype(bf16)
        snd[k, 1] = part[:, H:].astype(bf16)
        core_rs(k).start()
        here = pl.multiple_of(half * core, half)
        part = lax.dot_general(mixed_v[:, pl.ds(here, half)], g, dims, preferred_element_type=f32)
        acc[k, 0] = part[:, :H].astype(bf16)
        acc[k, 1] = part[:, H:].astype(bf16)

    def step(t, carry):
        when(t, 10, s10)
        when(t, 9, s9)
        when(t, 8, s8)
        when(t, 7, s7)
        when(t, 6, s6)
        when(t, 5, fold(b_rs, 3, rb, final))
        when(t, 4, fold(s_rs, 2, rs, lambda k, i: b_rs(k, i).start()))
        when(t, 3, fold(a_rs, 1, ra, lambda k, i: s_rs(k, i).start()))
        when(t, 2, fold(f_rs, 0, rf, lambda k, i: a_rs(k, i).start()))
        when(t, 1, s1)
        when(t, 0, compute)
        return carry

    def bias_hop(j):
        to = (pc, px, py, pz1, pz2)[j]
        return pltpu.make_async_remote_copy(
            gb_v.at[j], gr.at[j], bsem.at[j], brsem.at[j], device_id=(to,), device_id_type=MESH
        )

    lax.fori_loop(0, nch + 1, step, 0)
    for j in range(5):
        bias_hop(j).start()
        step(nch + 1 + j, 0)
        bias_hop(j).wait_recv()
        gb_v[j + 1] = gb_v[j] + gr[j]
    lax.fori_loop(nch + 6, nch + 11, step, 0)
    last = local(gb_v.at[5], gb, lsem.at[0])
    last.start()
    last.wait()
    for j in range(5):
        bias_hop(j).wait_send()
    act_out(nch - 2).wait()
    act_out(nch - 1).wait()

    def finish(k, carry):
        c = pl.multiple_of(k * CH, CH)
        local(gp_v.at[:, pl.ds(c, CH)], gp.at[:, pl.ds(c, CH)], gsem.at[k]).wait()
        core_rs(k).wait_send()
        for i in range(2):
            for f in (f_rs, a_rs, s_rs, b_rs, b_ag, s_ag, a_ag, f_ag, c_ag):
                f(k, i).wait_send()
        return carry

    lax.fori_loop(0, nch, finish, 0)


def main_call(mixed, weight, bias, cot):
    rows, width = mixed.shape
    nch = width // CH
    half = width // 2
    quart = half // 2
    any_ = pl.BlockSpec(memory_space=pl.ANY)
    dma = pltpu.SemaphoreType.DMA
    return pl.pallas_call(
        main_kernel,
        out_shape=(
            jax.ShapeDtypeStruct((rows, width), bf16),
            jax.ShapeDtypeStruct((rows, width), bf16),
            jax.ShapeDtypeStruct((2 * nch, width, H), bf16),
            jax.ShapeDtypeStruct((nch, CH), f32),
        ),
        in_specs=[any_] * 4,
        out_specs=[any_] * 4,
        scratch_shapes=[
            pltpu.VMEM((rows, width), bf16),
            pltpu.VMEM((width, width), bf16),
            pltpu.VMEM((nch, CH), f32),
            pltpu.VMEM((2, rows, CH), bf16),
            pltpu.VMEM((2, rows, CH), bf16),
            pltpu.VMEM((rows, width), bf16),
            pltpu.VMEM((8, 128), f32),
            pltpu.VMEM((nch, 2, half, H), bf16),
            pltpu.VMEM((nch, 2, half, H), bf16),
            pltpu.VMEM((nch, 2, half, H), bf16),
            pltpu.VMEM((nch, 2, quart, H), bf16),
            pltpu.VMEM((nch, 2, quart // 2, H), bf16),
            pltpu.VMEM((nch, 2, quart // 4, H), bf16),
            pltpu.VMEM((nch, 2, quart // 8, H), bf16),
            pltpu.VMEM((6, nch, CH), f32),
            pltpu.VMEM((5, nch, CH), f32),
            dma((2,)),
            dma((nch,)),
            dma((2,)),
            dma((2,)),
            dma((nch,)),
            dma((nch, 2)),
            dma((nch, 19)),
            dma((nch, 19)),
            dma((5,)),
            dma((5,)),
        ],
        compiler_params=pltpu.CompilerParams(
            collective_id=0, has_side_effects=True, vmem_limit_bytes=60 << 20
        ),
        name="layer",
    )(mixed, weight, bias.reshape(nch, CH), cot)


def widen_kernel(ag, out):
    for j in range(ag.shape[0]):
        out[:, j * H : (j + 1) * H] = ag[j].astype(f32)


def widen(ag):
    n, width, _ = ag.shape
    step = 256
    return pl.pallas_call(
        widen_kernel,
        out_shape=jax.ShapeDtypeStruct((width, n * H), f32),
        grid=(width // step,),
        in_specs=[pl.BlockSpec((n, step, H), lambda i: (0, i, 0))],
        out_specs=pl.BlockSpec((step, n * H), lambda i: (i, 0)),
        name="widen",
    )(ag)


def passed_along(value, axis, steps):
    count = lax.axis_size(axis)
    pairs = [(source, (source + steps) % count) for source in range(count)]
    return lax.ppermute(value, axis, pairs)


def tables(seg, offsets, marks, edges, edge_marks, rim):
    slots, rows = seg.shape
    order = jnp.arange(rows, dtype=jnp.int32)
    same = seg[:, :, None] == seg[:, None, :]
    start = jnp.min(jnp.where(same, order, rows), axis=2)
    extent = jnp.sum(same.astype(jnp.int32), axis=2)
    picks = jnp.where(marks == 1, offsets % extent[:, :, None], -1)
    lanes = jnp.arange(128, dtype=jnp.int32)
    near = jnp.sum((picks[:, :, :, None] == lanes).astype(f32), axis=2).astype(bf16)
    spread = (lanes[None, :, None] == (order - start)[:, None, :]).astype(bf16)
    local = jnp.einsum("sio,soj->sij", near, spread, preferred_element_type=f32)
    local = jnp.where(same, local, 0.0) + 2.0 * (order[:, None] == order[None, :])
    joined = jnp.concatenate([edges[:, 0], edges[:, 1] + rim], axis=2)
    joined_marks = jnp.concatenate([edge_marks[:, 0], edge_marks[:, 1]], axis=2)
    cols = jnp.arange(2 * rim, dtype=jnp.int32)
    far = jnp.sum(jnp.where(joined[..., None] == cols, joined_marks[..., None], 0), axis=2)
    degree = jnp.sum(marks, axis=2) + jnp.sum(joined_marks, axis=2)
    return local.astype(bf16), far.astype(bf16), 1.0 / (1.0 + degree.astype(f32))


def per_device(
    features,
    weight,
    bias,
    cotangent,
    segment_ids,
    neighbour_offsets,
    neighbour_mask,
    halo_edges,
    halo_mask,
    boundary_rows,
):
    slots, rows, width = features.shape
    rim = boundary_rows.shape[2]
    local_counts, halo_counts, scale = tables(
        segment_ids, neighbour_offsets, neighbour_mask, halo_edges, halo_mask, rim
    )
    chosen = (boundary_rows[..., None] == jnp.arange(rows, dtype=jnp.int32)).astype(bf16)
    sent = jnp.einsum("sjbr,srf->sjbf", chosen, features, preferred_element_type=f32).astype(bf16)
    from_prev = passed_along(sent[slots - 1, 1], "blk", 1)
    from_next = passed_along(sent[0, 0], "blk", -1)
    before = jnp.concatenate([from_prev[None], sent[: slots - 1, 1]], axis=0)
    after = jnp.concatenate([sent[1:, 0], from_next[None]], axis=0)
    received = jnp.concatenate([before, after], axis=1)
    summed = jnp.einsum("srk,skf->srf", local_counts, features, preferred_element_type=f32)
    summed = summed + jnp.einsum("srk,skf->srf", halo_counts, received, preferred_element_type=f32)
    mixed = (scale[:, :, None] * summed).astype(bf16).reshape(slots * rows, width)
    incoming = cotangent.reshape(slots * rows, width)
    if lax.axis_size("blk") == 32:
        activations, grad_pre, gathered, grad_bias = main_call(mixed, weight, bias, incoming)
        grad_weight = widen(gathered)
        grad_bias = grad_bias.reshape(-1)
    else:
        pre = jnp.dot(mixed, weight, preferred_element_type=f32) + bias[None, :]
        sigma = jax.nn.sigmoid(pre)
        activations = (pre * sigma).astype(bf16)
        grad_pre = (incoming.astype(f32) * (sigma * (1.0 + pre * (1.0 - sigma)))).astype(bf16)
        bias_term = jnp.sum(grad_pre, axis=0, dtype=f32)
        weight_term = lax.dot_general(
            mixed, grad_pre, (((0,), (0,)), ((), ())), preferred_element_type=f32
        )
        grad_weight, grad_bias = lax.psum((weight_term, bias_term), "blk")
    grad_mixed = lax.dot_general(
        grad_pre, weight, (((1,), (1,)), ((), ())), preferred_element_type=f32
    )
    grad_summed = (scale.reshape(-1)[:, None] * grad_mixed).astype(bf16)
    grad_summed = grad_summed.reshape(slots, rows, width)
    grad_received = jnp.einsum(
        "srk,srf->skf", halo_counts, grad_summed, preferred_element_type=f32
    ).astype(bf16)
    toward_prev = grad_received[:, :rim]
    toward_next = grad_received[:, rim:]
    back_prev = passed_along(toward_next[slots - 1], "blk", 1)
    back_next = passed_along(toward_prev[0], "blk", -1)
    grad_first = jnp.concatenate([back_prev[None], toward_next[: slots - 1]], axis=0)
    grad_second = jnp.concatenate([toward_prev[1:], back_next[None]], axis=0)
    grad_sent = jnp.stack([grad_first, grad_second], axis=1)
    grad_features = jnp.einsum(
        "srk,srf->skf", local_counts, grad_summed, preferred_element_type=f32
    ) + jnp.einsum("sjbr,sjbf->srf", chosen, grad_sent, preferred_element_type=f32)
    return (
        activations.reshape(slots, rows, width),
        grad_features.astype(bf16),
        grad_weight,
        grad_bias,
    )


def solution(mesh):
    in_specs = (
        P("blk", None, None),
        P(),
        P(),
        P("blk", None, None),
        P("blk", None),
        P("blk", None, None),
        P("blk", None, None),
        P("blk", None, None, None),
        P("blk", None, None, None),
        P("blk", None, None),
    )
    out_specs = (P("blk", None, None), P("blk", None, None), P(), P())
    return jax.shard_map(
        per_device, mesh=mesh, in_specs=in_specs, out_specs=out_specs, check_vma=False
    )
```

time: 453 us -> 216 us (0.48)
  other arithmetic: 180 us -> 33 us
  Pallas kernels: 0 us -> 113 us
  waiting for transfers between devices: 98.6 us -> 0.01 us
  blocking collectives: 38.6 us -> 0 us
  local copies, waits for them, and re-layouts: 35.2 us -> 9 us
  matrix products: 72.1 us -> 47.3 us
  between operations: 14.2 us -> 0.94 us
    pallas_call x0 -> x2, Pallas kernels: none -> 113 us  [the longest x1 103 us: main_call(): pl.pallas_call(main_kernel, out_shape=(jax.ShapeDtypeStruct((rows, width)...]
    scatter-add x2 -> x0, other arithmetic: 98.9 us -> none  [per_device(): block.at[picks.reshape(-1)].add(values.reshape(-1, values.shape[-1]))]
    psum x1 -> x0, waiting for transfers between devices: 98.6 us -> none  [per_device(): grad_weight, grad_bias = lax.psum((weight_term, bias_term), 'blk')]
    psum x1 -> x0, blocking collectives: 38.6 us -> none  [per_device(): grad_weight, grad_bias = lax.psum((weight_term, bias_term), 'blk')]
    dot_general x2 -> x3, matrix products: 38.3 us -> 13.1 us  [the longest x1 7.12 us: per_device(): jnp.einsum('sjbr,sjbf->srf', chosen, grad_sent, preferred_element_type=f32)]
    reduce_sum x16 -> x5, other arithmetic: 53.3 us -> 29.8 us  [the longest x1 15.8 us: tables(): jnp.sum((picks[:, :, :, None] == lanes).astype(f32), axis=2).astype(bf16)]
    unnamed x11 -> x30, local copies, waits for them, and re-layouts: 14.9 us -> 4.04 us
    gather x2 -> x0, local copies, waits for them, and re-layouts: 10.1 us -> none  [per_device(): sent = jax.vmap(lambda block, picks: block[picks])(features, boundary_rows)]
  transfers between devices with their start and end apart: 5 -> 4, of which waited for: 1 -> 0; matrix products, arithmetic and copies ran while one was open for 49% -> 21% of each run, Pallas kernels for 0% -> 5%
where the time goes in v1:
time: 216 us; the launch traced here: 215 us
  Pallas kernels  113 us (52%)
  matrix products  47.3 us (22%)
  other arithmetic  33 us (15%)
  starting transfers between devices  11.9 us (6%)
  local copies, waits for them, and re-layouts  9 us (4%)
    pallas_call x1, Pallas kernels, main_call(): pl.pallas_call(main_kernel, out_shape=(jax.ShapeDtypeStruct((rows, width)...  103 us
    dot_general x1, matrix products, per_device(): lax.dot_general(grad_pre, weight, (((1,), (1,)), ((), ())), preferred_ele...  16.3 us
    reduce_sum x1, other arithmetic, tables(): jnp.sum((picks[:, :, :, None] == lanes).astype(f32), axis=2).astype(bf16)  15.8 us
    ppermute x4, starting transfers between devices, passed_along(): return lax.ppermute(value, axis, pairs)  11.9 us
    pallas_call x1, Pallas kernels, widen(): pl.pallas_call(widen_kernel, out_shape=jax.ShapeDtypeStruct((width, n * H...  10.7 us
    reduce_sum x1, other arithmetic, tables(): jnp.sum(jnp.where(joined[..., None] == cols, joined_marks[..., None], 0),...  8.64 us
    dot_general x1, matrix products, per_device(): jnp.einsum('sjbr,sjbf->srf', chosen, grad_sent, preferred_element_type=f32)  7.12 us
    dot_general x1, matrix products, per_device(): jnp.einsum('srk,srf->skf', local_counts, grad_summed, preferred_element_t...  6.35 us
  transfers between devices with their start and end apart: 4, of which 0 were waited for; matrix products, arithmetic and copies ran while one was open for 21% of the time, Pallas kernels for 5%

profile of v1, /device:TPU:0, one launch (start us, length us, event | category | flops | bytes accessed | tf_op | source)
XLA Modules:
  0.0 215.4 jit_solution(6148143945351344572)
XLA Ops:
  0.7 4.0 %fusion.3 = bf16[4,2,64,2048]{3,2,1,0:T(8,128)(2,1)S(1)} fusion(bf16[4,352,2048]{2,1,0:T(8,128)(2,1)} %param.10, s32[4,2,64]{2,1,0:T(2,128)} %param.19), kind=kOutput, calls=%fused_computation.13 | convolution fusion | flops 739426304 | bytes 7866368 | tf_op jit(solution)/shard_map/sjbr,srf->sjbf/dot_general | solution.py:383
  4.7 0.8 slice_bitcast_fusion.5
  6.0 5.9 %collective-permute-start.1 = (bf16[64,2048]{1,0:T(8,128)(2,1)}, bf16[64,2048]{1,0:T(8,128)(2,1)}, u32[]{:S(2)}, u32[]{:S(2)}) collective-permute-start(bf16[64,2048]{1,0:T(8,128)(2,1)} %get-tuple-element.19), channel_id=1, source_target_pairs={{0,31},{1,0},{2,1},{3,2},{4,3},{5,4},{6,5},{7,6},{8,7},{9,8},{10,9... | collective-permute-start | bytes 786440 | tf_op jit(solution)/shard_map/ppermute | solution.py:342
  12.0 0.8 fusion.18
  13.4 0.8 fusion.6
  15.5 4.6 %fusion.28 = (s32[4,352]{1,0:T(4,128)S(1)}, s32[4,352,64]{1,2,0:T(8,128)}) fusion(s32[4,352,64]{1,2,0:T(8,128)S(1)} %copy-done.3, pred[4,352]{1,0:T(4,128)(4,1)S(1)} %broadcast_compare_fusion, s32[4,352,64]{1,2,0:T(8,128)S(1)} %copy-done.4, s32[4,352]{1,0:T(4,128)S(1)} %get-tuple-element.29), kind=kLoop, calls=%fused_computation.62 | loop fusion | flops 899712 | bytes 1094016 | tf_op jit(solution)/shard_map/reduce_sum | solution.py:361
  21.1 0.8 pad_add_fusion
  21.9 1.1 copy.25
  23.0 1.2 copy.23
  24.3 15.8 %convert_reduce_fusion = bf16[4,352,128]{2,1,0:T(8,128)(2,1)S(1)} fusion(s32[4,352,64]{2,1,0:T(8,128)S(1)} %copy.23), kind=kLoop, calls=%fused_computation | loop fusion | flops 34422784 | bytes 720896 | tf_op jit(solution)/shard_map/reduce_sum | solution.py:353
  40.0 1.9 fusion.9
  42.0 5.6 %fusion.29 = f32[4,352,2048]{2,1,0:T(8,128)S(1)} fusion(bf16[4,352,352]{2,1,0:T(8,128)(2,1)S(1)} %fusion.9, bf16[4,352,2048]{2,1,0:T(8,128)(2,1)} %param.10), kind=kOutput, calls=%fused_computation.63 | convolution fusion | flops 2030043136 | bytes 18292736 | tf_op jit(solution)/shard_map/srk,skf->srf/dot_general | solution.py:389
  47.7 8.6 %select_reduce_fusion = s32[4,352,128]{2,1,0:T(8,128)S(1)} fusion(s32[4,352,16]{2,1,0:T(8,128)S(1)} %copy.26, s32[4,352,16]{2,1,0:T(8,128)S(1)} %copy-done.2), kind=kLoop, calls=%fused_computation.6 | loop fusion | flops 8470528 | bytes 901120 | tf_op jit(solution)/shard_map/reduce_sum | solution.py:360
  56.4 4.6 %multiply_convert_fusion.1 = bf16[4,352,2048]{2,1,0:T(8,128)(2,1)} fusion(f32[4,352,2048]{2,1,0:T(8,128)S(1)} %fusion.29, f32[4,352]{1,0:T(4,128)S(1)} %add_divide_fusion, bf16[1,64,2048]{2,1,0:T(8,128)(2,1)} %bitcast.11, bf16[3,64,2048]{2,1,0:T(8,128)(2,1)S(1)} %get-tuple-element.21, bf16[3,64,2048]{2,1,0:T(8,128)(2,1)S(1)} %get-tuple-element.20, ...), kind=kOutput, calls=%fused_computation.5 | convolution fusion | flops 755417088 | bytes 20125184 | tf_op jit(solution)/shard_map/srk,skf->srf/dot_general | solution.py:390
  61.0 102.6 %layer.1 = (bf16[1408,2048]{1,0:T(8,128)(2,1)}, bf16[1408,2048]{1,0:T(8,128)(2,1)}, bf16[16,2048,128]{2,1,0:T(8,128)(2,1)}, f32[8,256]{1,0:T(8,128)}) custom-call(bf16[1408,2048]{1,0:T(8,128)(2,1)} %bitcast.63, bf16[2048,2048]{1,0:T(8,128)(2,1)} %w.1, f32[8,256]{1,0:T(8,128)} %reshape.99.bias, bf16[1408,2048]{1,0:T(8,128)(2,1)} %bitcast.67), custom_call_target="tpu_custom_call" | custom-call | tf_op jit(solution)/shard_map/layer/pallas_call | solution.py:276
  163.6 16.3 %multiply_convert_fusion = bf16[1408,2048]{1,0:T(8,128)(2,1)S(1)} fusion(bf16[1408,2048]{1,0:T(8,128)(2,1)} %get-tuple-element.9, bf16[2048,2048]{1,0:T(8,128)(2,1)} %w.1, f32[1408]{0:T(1024)S(1)} %copy-done.9), kind=kOutput, calls=%fused_computation.4 | convolution fusion | flops 11816927232 | bytes 19928576 | tf_op jit(solution)/shard_map/dot_general | solution.py:407
  180.0 1.3 convolution_convert_fusion
  181.3 6.3 %fusion.30 = f32[4,352,2048]{2,1,0:T(8,128)} fusion(bf16[4,352,352]{2,1,0:T(8,128)(2,1)S(1)} %copy-done.1, bf16[4,352,2048]{2,1,0:T(8,128)(2,1)S(1)} %bitcast.62), kind=kOutput, calls=%fused_computation.64 | convolution fusion | flops 2030043136 | bytes 18292736 | tf_op jit(solution)/shard_map/srk,srf->skf/dot_general | solution.py:422
  187.7 1.3 collective-permute-start.2
  189.0 4.2 %collective-permute-start.3 = (bf16[64,2048]{1,0:T(8,128)(2,1)S(1)}, bf16[64,2048]{1,0:T(8,128)(2,1)S(1)}, u32[]{:S(2)}, u32[]{:S(2)}) collective-permute-start(bf16[64,2048]{1,0:T(8,128)(2,1)S(1)} %get-tuple-element.15), channel_id=1, source_target_pairs={{0,31},{1,0},{2,1},{3,2},{4,3},{5,4},{6,5},{7,6},{8,7},{9,8},{10,9... | collective-permute-start | bytes 786440 | tf_op jit(solution)/shard_map/ppermute | solution.py:342
  194.0 10.7 %widen.1 = f32[2048,2048]{1,0:T(8,128)} custom-call(bf16[16,2048,128]{2,1,0:T(8,128)(2,1)} %get-tuple-element.10.ag), custom_call_target="tpu_custom_call" | custom-call | tf_op jit(solution)/shard_map/widen/pallas_call | solution.py:329
  204.9 7.1 %fusion = bf16[4,352,2048]{2,1,0:T(8,128)(2,1)} fusion(f32[4,352,2048]{2,1,0:T(8,128)} %fusion.30, s32[4,2,64]{2,1,0:T(2,128)S(1)} %copy-done.8, bf16[4,1,64,2048]{3,2,0,1:T(8,128)(2,1)S(1)} %maximum_bitcast_fusion.1, bf16[4,1,64,2048]{3,2,0,1:T(8,128)(2,1)S(1)} %maximum_bitcast_fusion), kind=kOutput, calls=%fused_computation.3 | convolution fusion | flops 745193472 | bytes 19400704 | tf_op jit(solution)/shard_map/sjbr,sjbf->srf/dot_general | solution.py:424
  212.1 0.8 slice-done.1
  212.9 2.5 %copy.40 = bf16[4,352,2048]{2,1,0:T(8,128)(2,1)} copy(bf16[4,352,2048]{2,1,0:T(8,128)(2,1)S(1)} %bitcast.66) | data formatting | bytes 11534336
  (49 shorter events, 4.4 us)
Async XLA Ops:
  0.6 11.3 %copy-start.5 = (s32[4,2,352,8]{2,3,1,0:T(8,128)S(1)}, s32[4,2,352,8]{2,3,1,0:T(8,128)}, u32[]{:S(2)}) copy-start(s32[4,2,352,8]{2,3,1,0:T(8,128)} %param.18) | copy-start | bytes 270340
  0.6 12.2 %copy-start.10 = (f32[2048]{0:T(1024)S(1)}, f32[2048]{0:T(1024)}, u32[]{:S(2)}) copy-start(f32[2048]{0:T(1024)} %param.12) | copy-start | bytes 24580
  0.7 12.8 %copy-start.7 = (s32[4,352]{1,0:T(4,128)S(1)}, s32[4,352]{1,0:T(4,128)}, u32[]{:S(2)}) copy-start(s32[4,352]{1,0:T(4,128)} %param.14) | copy-start | bytes 16900
  0.7 14.2 %copy-start.6 = (s32[4,2,352,8]{2,3,1,0:T(8,128)S(1)}, s32[4,2,352,8]{2,3,1,0:T(8,128)}, u32[]{:S(2)}) copy-start(s32[4,2,352,8]{2,3,1,0:T(8,128)} %param.17) | copy-start | bytes 270340
  0.7 14.9 %copy-start.3 = (s32[4,352,64]{1,2,0:T(8,128)S(1)}, s32[4,352,64]{1,2,0:T(8,128)}, u32[]{:S(2)}) copy-start(s32[4,352,64]{1,2,0:T(8,128)} %param.16) | copy-start | bytes 1081348
  0.7 14.9 %copy-start.4 = (s32[4,352,64]{1,2,0:T(8,128)S(1)}, s32[4,352,64]{1,2,0:T(8,128)}, u32[]{:S(2)}) copy-start(s32[4,352,64]{1,2,0:T(8,128)} %param.15) | copy-start | bytes 1081348
  5.6 50.9 %collective-permute-start = (bf16[64,2048]{1,0:T(8,128)(2,1)}, bf16[64,2048]{1,0:T(8,128)(2,1)}, u32[]{:S(2)}, u32[]{:S(2)}) collective-permute-start(bf16[64,2048]{1,0:T(8,128)(2,1)} %get-tuple-element.18), channel_id=1, source_target_pairs={{0,1},{1,2},{2,3},{3,4},{4,5},{5,6},{6,7},{7,8},{8,9},{9,10},{10,1... | collective-permute-start | bytes 786440 | tf_op jit(solution)/shard_map/ppermute | solution.py:342
  6.0 50.4 %collective-permute-start.1 = (bf16[64,2048]{1,0:T(8,128)(2,1)}, bf16[64,2048]{1,0:T(8,128)(2,1)}, u32[]{:S(2)}, u32[]{:S(2)}) collective-permute-start(bf16[64,2048]{1,0:T(8,128)(2,1)} %get-tuple-element.19), channel_id=1, source_target_pairs={{0,31},{1,0},{2,1},{3,2},{4,3},{5,4},{6,5},{7,6},{8,7},{9,8},{10,9... | collective-permute-start | bytes 786440 | tf_op jit(solution)/shard_map/ppermute | solution.py:342
  42.0 5.7 %copy-start = (bf16[4,352,352]{2,1,0:T(8,128)(2,1)}, bf16[4,352,352]{2,1,0:T(8,128)(2,1)S(1)}, u32[]{:S(2)}) copy-start(bf16[4,352,352]{2,1,0:T(8,128)(2,1)S(1)} %fusion.9) | copy-start | bytes 2973700
  42.0 5.7 %copy-start.2 = (s32[4,352,16]{2,1,0:T(8,128)S(1)}, s32[4,352,16]{2,1,0:T(8,128)}, u32[]{:S(2)}) copy-start(s32[4,352,16]{2,1,0:T(8,128)} %copy.25) | copy-start | bytes 270340
  61.0 102.6 %copy-start.9 = (f32[1408]{0:T(1024)S(1)}, f32[1408]{0:T(1024)}, u32[]{:S(2)}) copy-start(f32[1408]{0:T(1024)} %reshape.105) | copy-start | bytes 16900
  180.0 1.3 copy-start.1
  181.3 12.0 %copy-start.11 = (f32[8,256]{1,0:T(8,128)S(1)}, f32[8,256]{1,0:T(8,128)}, u32[]{:S(2)}) copy-start(f32[8,256]{1,0:T(8,128)} %get-tuple-element.11) | copy-start | bytes 24580
  187.7 17.0 %collective-permute-start.2 = (bf16[64,2048]{1,0:T(8,128)(2,1)S(1)}, bf16[64,2048]{1,0:T(8,128)(2,1)S(1)}, u32[]{:S(2)}, u32[]{:S(2)}) collective-permute-start(bf16[64,2048]{1,0:T(8,128)(2,1)S(1)} %get-tuple-element.14), channel_id=1, source_target_pairs={{0,1},{1,2},{2,3},{3,4},{4,5},{5,6},{6,7},{7,8},{8,9},{9,10},{10,1... | collective-permute-start | bytes 786440 | tf_op jit(solution)/shard_map/ppermute | solution.py:342
  189.0 15.8 %collective-permute-start.3 = (bf16[64,2048]{1,0:T(8,128)(2,1)S(1)}, bf16[64,2048]{1,0:T(8,128)(2,1)S(1)}, u32[]{:S(2)}, u32[]{:S(2)}) collective-permute-start(bf16[64,2048]{1,0:T(8,128)(2,1)S(1)} %get-tuple-element.15), channel_id=1, source_target_pairs={{0,31},{1,0},{2,1},{3,2},{4,3},{5,4},{6,5},{7,6},{8,7},{9,8},{10,9... | collective-permute-start | bytes 786440 | tf_op jit(solution)/shard_map/ppermute | solution.py:342
  194.0 11.0 %copy-start.8 = (s32[4,2,64]{2,1,0:T(2,128)S(1)}, s32[4,2,64]{2,1,0:T(2,128)}, u32[]{:S(2)}) copy-start(s32[4,2,64]{2,1,0:T(2,128)} %param.19) | copy-start | bytes 6148
  204.8 7.3 %slice-start = ((s8[5767168]{0:T(1024)(128)(4,1)}), s8[4194304]{0:T(1024)(128)(4,1)S(1)}, s32[]{:S(2)}) async-start(s8[5767168]{0:T(1024)(128)(4,1)} %bitcast.64), calls=%async_computation | async-start | bytes 8388608
  204.9 8.0 %slice-start.1 = ((s8[5767168]{0:T(1024)(128)(4,1)}), s8[1572864]{0:T(1024)(128)(4,1)S(1)}, s32[]{:S(2)}) async-start(s8[5767168]{0:T(1024)(128)(4,1)} %bitcast.64), calls=%async_computation.1 | async-start | bytes 3145728

commit v2 on v1

v2 whole, which is shorter than its diff:
```python
import functools

import jax
import jax.numpy as jnp
from jax import lax
from jax.experimental import pallas as pl
from jax.experimental.pallas import tpu as pltpu
from jax.sharding import PartitionSpec as P

bf16 = jnp.bfloat16
f32 = jnp.float32
MESH = pl.DeviceIdType.MESH
CH = 256
H = 128


def neighbours(me):
    core = me % 2
    bits = [core, (me // 2) % 2, (me // 4) % 2, (me // 8) % 2, me // 16]
    return bits, [me + (1 << i) - (2 << i) * b for i, b in enumerate(bits)]


def main_kernel(
    x, w, bias, cot, seg, offs, marks, edges, edge_marks, rims,
    act, gf, ag, gb,
    xr, kt, ot, sc, mixed_v, w_v, bias_v, cot_v, act_v, gp_v,
    seg_v, offs_v, marks_v, edges_v, emarks_v, rims_v, qv, vv, hs, hr,
    snd, rc, acc, rf, ra, rs, rb, gb_v, gr,
    xsem, tsem, wsem, csem, asem, fsem, ksem, ssem, rsem, bsem, brsem, hsem, hrsem,
):
    n = lax.axis_size("blk")
    me = lax.axis_index("blk")
    slots, deep, width = xr.shape
    rows = kt.shape[2]
    rim = rims_v.shape[2]
    near = offs_v.shape[2]
    halo = edges_v.shape[3]
    total = slots * rows
    nch = width // CH
    half = width // 2
    unit = half // U
    (core, bx, by, bz1, bz2), (pc, px, py, pz1, pz2) = neighbours(me)
    prev = lax.rem(me + n - 1, n)
    nxt = lax.rem(me + 1, n)
    first = [px * (1 - core) + py * core, py * (1 - core) + px * core]
    fbit = [bx * (1 - core) + by * core, by * (1 - core) + bx * core]
    second = [first[1], first[0]]
    sbit = [fbit[1], fbit[0]]

    barrier = pltpu.get_barrier_semaphore()
    for p in (pc, px, py, pz1, pz2, prev, nxt):
        pl.semaphore_signal(barrier, inc=1, device_id=(p,), device_id_type=MESH)

    def local(src, dst, sem):
        return pltpu.make_async_copy(src, dst, sem)

    def cols(k):
        return pl.ds(pl.multiple_of(k * CH, CH), CH)

    def slot_rows(s):
        return pl.ds(pl.multiple_of(s * rows, 16), rows)

    def x_in(s):
        return local(x.at[slot_rows(s)], xr.at[s, pl.ds(0, rows)], xsem.at[s])

    def w_in(k):
        return local(w.at[:, cols(k)], w_v.at[:, cols(k)], wsem.at[k])

    def cot_in(k):
        return local(cot.at[:, cols(k)], cot_v.at[k % 2], csem.at[k % 2])

    def act_out(k):
        return local(act_v.at[k % 2], act.at[:, cols(k)], asem.at[k % 2])

    def gf_out(s):
        return local(xr.at[s, pl.ds(0, rows)], gf.at[slot_rows(s)], fsem.at[s])

    small = [
        local(src, dst, tsem.at[i])
        for i, (src, dst) in enumerate(
            (
                (rims, rims_v),
                (seg, seg_v),
                (offs, offs_v),
                (marks, marks_v),
                (edges, edges_v),
                (edge_marks, emarks_v),
                (bias, bias_v),
            )
        )
    ]
    small[0].start()
    x_in(0).start()
    x_in(slots - 1).start()
    for c in small[1:]:
        c.start()
    for s in range(1, slots - 1):
        x_in(s).start()
    w_in(0).start()
    cot_in(0).start()
    cot_in(1).start()
    for k in range(1, nch):
        w_in(k).start()

    def offer(s):
        picks = jnp.concatenate([rims_v[s, 0:1, :], rims_v[s, 1:2, :]], axis=1)
        order = lax.broadcasted_iota(jnp.int32, (rows, 2 * rim), 0)
        ot[s] = jnp.where(order == picks, 1.0, 0.0).astype(bf16)
        dims = (((0,), (0,)), ((), ()))
        return lax.dot_general(
            ot[s], xr[s, pl.ds(0, rows), :], dims, preferred_element_type=f32
        ).astype(bf16)

    def halo_send(j):
        s, to = ((0, nxt), (slots - 1, prev))[j]
        dst = xr.at[s, pl.ds(rows + rim * j, rim)]
        return pltpu.make_async_remote_copy(
            hs.at[j], dst, hsem.at[j], hrsem.at[j], device_id=(to,), device_id_type=MESH
        )

    def back_send(j):
        to = (prev, nxt)[j]
        return pltpu.make_async_remote_copy(
            hs.at[2 + j], hr.at[j], hsem.at[2 + j], hrsem.at[2 + j],
            device_id=(to,), device_id_type=MESH,
        )

    small[0].wait()
    x_in(0).wait()
    out = offer(0)
    hs[1] = out[:rim]
    xr[1, pl.ds(rows, rim), :] = out[rim:]
    x_in(slots - 1).wait()
    out = offer(slots - 1)
    hs[0] = out[rim:]
    xr[slots - 2, pl.ds(rows + rim, rim), :] = out[:rim]
    pl.semaphore_wait(barrier, 7)
    halo_send(0).start()
    halo_send(1).start()
    for c in small[1:]:
        c.wait()
    for s in range(1, slots - 1):
        x_in(s).wait()
        out = offer(s)
        xr[s - 1, pl.ds(rows + rim, rim), :] = out[:rim]
        xr[s + 1, pl.ds(rows, rim), :] = out[rim:]

    def eye(size):
        r = lax.broadcasted_iota(jnp.int32, (size, size), 0)
        c = lax.broadcasted_iota(jnp.int32, (size, size), 1)
        return jnp.where(r == c, 1.0, 0.0).astype(bf16)

    def turned(value):
        dims = (((1,), (1,)), ((), ()))
        return lax.dot_general(
            eye(value.shape[1]), value.astype(bf16), dims, preferred_element_type=f32
        ).astype(jnp.int32)

    def tables(s, carry):
        seg_r = seg_v[pl.ds(s, 1), :].astype(f32)
        ri = lax.broadcasted_iota(jnp.int32, (rows, rows), 0)
        ci = lax.broadcasted_iota(jnp.int32, (rows, rows), 1)
        diag = ri == ci
        seg_c = jnp.sum(jnp.where(diag, seg_r, 0.0), axis=1, keepdims=True)
        start = jnp.sum(jnp.where(seg_r < seg_c, 1.0, 0.0), axis=1, keepdims=True)
        same = seg_r == seg_c
        size = jnp.sum(jnp.where(same, 1.0, 0.0), axis=1, keepdims=True)
        off = offs_v[s].astype(f32)
        rest = off - jnp.floor((off + 0.5) * (1.0 / size)) * size
        rest = jnp.where(rest < 0.0, rest + size, rest)
        rest = jnp.where(rest >= size, rest - size, rest)
        marked = marks_v[s]
        pick = turned(jnp.where(marked == 1, rest, 200.0))
        qv[...] = pick >> 2
        vv[...] = 1 << ((pick & 3) << 3)
        q = lax.broadcasted_iota(jnp.int32, (Q, rows), 0)
        packed = jnp.zeros((Q, rows), jnp.int32)
        for k in range(near):
            packed = packed + jnp.where(qv[k : k + 1, :] == q, vv[k : k + 1, :], 0)
        counts = jnp.concatenate(
            [((packed >> (8 * r)) & 255).astype(f32) for r in range(4)], axis=0
        ).astype(bf16)
        rel = lax.broadcasted_iota(jnp.int32, (rows, 1), 0) - start.astype(jnp.int32)
        place = (rel & 3) * Q + (rel >> 2)
        lanes = lax.broadcasted_iota(jnp.int32, (rows, 4 * Q), 1)
        spread = jnp.where(lanes == place, 1.0, 0.0).astype(bf16)
        around = jnp.dot(spread, counts, preferred_element_type=f32)
        around = jnp.where(same, around, 0.0) + jnp.where(diag, 2.0, 0.0)
        kt[s, pl.ds(0, rows), :] = around.astype(bf16)
        degree = jnp.sum(marked.astype(f32), axis=1, keepdims=True)
        r = lax.broadcasted_iota(jnp.int32, (rim, rows), 0)
        for j in range(2):
            hot = emarks_v[s, j]
            degree = degree + jnp.sum(hot.astype(f32), axis=1, keepdims=True)
            pick = turned(jnp.where(hot == 1, edges_v[s, j].astype(f32), 200.0))
            far = jnp.zeros((rim, rows), f32)
            for k in range(halo):
                far = far + jnp.where(pick[k : k + 1, :] == r, 1.0, 0.0)
            kt[s, pl.ds(rows + rim * j, rim), :] = far.astype(bf16)
        sc[slot_rows(s), :] = 1.0 / (1.0 + degree)
        return carry

    lax.fori_loop(0, slots, tables, 0)

    def mix(s):
        d = slot_rows(s)
        dims = (((0,), (0,)), ((), ()))
        for j in range(4):
            c = pl.ds(j * (width // 4), width // 4)
            summed = lax.dot_general(kt[s], xr[s, :, c], dims, preferred_element_type=f32)
            mixed_v[d, c] = (sc[d, :] * summed).astype(bf16)

    for s in range(1, slots - 1):
        mix(s)
    halo_send(0).wait_recv()
    halo_send(1).wait_recv()
    mix(0)
    mix(slots - 1)

    def remote(src, dst, k, s, to):
        return pltpu.make_async_remote_copy(
            src, dst, ssem.at[k, s], rsem.at[k, s], device_id=(to,), device_id_type=MESH
        )

    def at(u, level, flip=False, base=0):
        r = base + unit * u
        size = unit
        picks = [bz1, sbit[u % 2]]
        for j in range(level):
            size = size // 2
            b = picks[j]
            if flip and j == level - 1:
                b = 1 - b
            r = r + size * b
        return pl.ds(pl.multiple_of(r, 16), size)

    def c_rs(k, u):
        return remote(snd.at[k % 2, :, at(u, 0)], rc.at[k, :, at(u, 0)], k, u, pc)

    def f_rs(k, u):
        f = fbit[u % 2]
        return remote(acc.at[k, 1 - f, at(u, 0)], rf.at[k, u], k, U + u, first[u % 2])

    def a_rs(k, u):
        return remote(acc.at[k, fbit[u % 2], at(u, 1, True)], ra.at[k, u], k, 2 * U + u, pz1)

    def s_rs(k, u):
        f = fbit[u % 2]
        return remote(acc.at[k, f, at(u, 2, True)], rs.at[k, u], k, 3 * U + u, second[u % 2])

    def b_rs(k, u):
        return remote(acc.at[k, fbit[u % 2], at(u, 2)], rb.at[k, u], k, 4 * U + u, pz2)

    def ag_at(k, u, level):
        return ag.at[2 * k + fbit[u % 2], at(u, level, False, half * core)]

    def keep(k, u):
        return local(rs.at[k, u], ag_at(k, u, 2), ksem.at[k, u])

    def s_ag(k, u):
        return remote(rs.at[k, u], ag_at(k, u, 2), k, 5 * U + u, second[u % 2])

    def a_ag(k, u):
        return remote(ag_at(k, u, 1), ag_at(k, u, 1), k, 6 * U + u, pz1)

    def f_ag(k, u):
        return remote(ag_at(k, u, 0), ag_at(k, u, 0), k, 7 * U + u, first[u % 2])

    def c_ag(k, u):
        part = ag.at[pl.ds(2 * k, 2), at(u, 0, False, half * core)]
        return remote(part, part, k, 8 * U + u, pc)

    def fold(level, buf):
        def run(k, u):
            f = fbit[u % 2]
            d = at(u, level)
            acc[k, f, d] = acc[k, f, d] + buf[k, u]

        return run

    def fold_core(k, u):
        d = at(u, 0)
        for j in range(2):
            acc[k, j, d] = acc[k, j, d] + rc[k, j, d]

    def last_fold(k, u):
        rs[k, u] = acc[k, fbit[u % 2], at(u, 2)] + rb[k, u]
        keep(k, u).start()

    def settle(k, u):
        keep(k, u).wait()

    hops = [
        (c_rs, fold_core, f_rs),
        (f_rs, fold(0, rf), a_rs),
        (a_rs, fold(1, ra), s_rs),
        (s_rs, fold(2, rs), b_rs),
        (b_rs, last_fold, s_ag),
        (s_ag, settle, a_ag),
        (a_ag, None, f_ag),
        (f_ag, None, c_ag),
        (c_ag, None, None),
    ]

    def serve(t, v, order):
        for h in order:
            took, work, send = hops[h]
            back = v - DELAY[h]
            k = t + back // U
            u = back % U

            @pl.when((k >= 0) & (k < nch))
            def _():
                took(k, u).wait_recv()
                if work is not None:
                    work(k, u)
                if send is not None:
                    send(k, u).start()

    def pre_part(k, m):
        mt = total // 2
        d = pl.ds(m * mt, mt)
        b = bias_v[pl.ds(k, 1), :]
        pre = jnp.dot(mixed_v[d, :], w_v[:, cols(k)], preferred_element_type=f32) + b
        sig = 0.5 * jnp.tanh(0.5 * pre) + 0.5
        out = pre * sig
        act_v[k % 2, d, :] = out.astype(bf16)
        g = (cot_v[k % 2, d, :].astype(f32) * (sig + out * (1.0 - sig))).astype(bf16)
        gp_v[d, cols(k)] = g
        sums = jnp.sum(g.astype(f32), axis=0, keepdims=True)
        if m:
            sums = sums + gb_v[0, pl.ds(k, 1), :]
        gb_v[0, pl.ds(k, 1), :] = sums

    def grad_part(k, side):
        start = pl.multiple_of(half * side, half)
        dims = (((0,), (0,)), ((), ()))
        return lax.dot_general(
            mixed_v[:, pl.ds(start, half)], gp_v[:, cols(k)], dims, preferred_element_type=f32
        )

    def there(k):
        part = grad_part(k, 1 - core)
        snd[k % 2, 0] = part[:, :H].astype(bf16)
        snd[k % 2, 1] = part[:, H:].astype(bf16)

    def here(k):
        part = grad_part(k, core)
        acc[k, 0] = part[:, :H].astype(bf16)
        acc[k, 1] = part[:, H:].astype(bf16)

    def early(t, more):
        serve(t, 0, ORDER)
        serve(t, 1, ORDER)

        @pl.when(t >= 2)
        def _():
            for u in range(U):
                c_rs(t - 2, u).wait_send()

        if more:
            w_in(t + 1).wait()
            cot_in(t + 1).wait()

            @pl.when(t >= 1)
            def _():
                act_out(t - 1).wait()

        there(t)
        if more:
            pre_part(t + 1, 0)
        for u in range(U):
            c_rs(t, u).start()
        serve(t, 2, ORDER)
        serve(t, 3, ORDER)
        here(t)
        if more:
            pre_part(t + 1, 1)
            act_out(t + 1).start()

            @pl.when(t + 2 < nch)
            def _():
                cot_in(t + 2).start()

    w_in(0).wait()
    cot_in(0).wait()
    pre_part(0, 0)
    pre_part(0, 1)
    act_out(0).start()

    def early_step(t, carry):
        early(t, True)
        return carry

    lax.fori_loop(0, nch - 1, early_step, 0)
    early(nch - 1, False)

    def bias_hop(j):
        to = pc
        for i, p in enumerate((px, py, pz1, pz2)):
            to = jnp.where(j == i + 1, p, to)
        return pltpu.make_async_remote_copy(
            gb_v.at[j], gr.at[j], bsem.at[j], brsem.at[j], device_id=(to,), device_id_type=MESH
        )

    def bias_step(i):
        @pl.when((i >= 1) & (i <= 5))
        def _():
            bias_hop(i - 1).wait_recv()
            gb_v[i] = gb_v[i - 1] + gr[i - 1]

        @pl.when(i < 5)
        def _():
            bias_hop(i).start()

    def late_mixed(i, carry):
        bias_step(i)
        s = jnp.where(i == 0, 0, jnp.where(i == 1, slots - 1, i - 1))
        d = slot_rows(s)
        tile = width // 4
        for v in range(U):
            serve(nch + i, v, ORDER)
            c = pl.ds(v * tile, tile)
            dims = (((1,), (1,)), ((), ()))
            back = lax.dot_general(gp_v[d, :], w_v[c, :], dims, preferred_element_type=f32)
            mixed_v[d, c] = (sc[d, :] * back).astype(bf16)
        out = jnp.dot(
            kt[s, pl.ds(rows, 2 * rim), :], mixed_v[d, :], preferred_element_type=f32
        ).astype(bf16)

        @pl.when(s > 0)
        def _():
            xr[s - 1, pl.ds(rows + rim, rim), :] = out[:rim]

        @pl.when(s < slots - 1)
        def _():
            xr[s + 1, pl.ds(rows, rim), :] = out[rim:]

        @pl.when(s == 0)
        def _():
            hs[2] = out[:rim]
            back_send(0).start()

        @pl.when(s == slots - 1)
        def _():
            hs[3] = out[rim:]
            back_send(1).start()

        return carry

    lax.fori_loop(0, slots, late_mixed, 0)
    back_send(0).wait_recv()
    back_send(1).wait_recv()
    xr[slots - 1, pl.ds(rows + rim, rim), :] = hr[0]
    xr[0, pl.ds(rows, rim), :] = hr[1]

    def late_features(s, carry):
        bias_step(s + slots)
        d = slot_rows(s)
        tile = width // 4
        for v in range(U):
            serve(nch + slots + s, v, ORDER)
            c = pl.ds(v * tile, tile)
            grad = jnp.dot(kt[s, pl.ds(0, rows), :], mixed_v[d, c], preferred_element_type=f32)
            grad = grad + jnp.dot(
                ot[s], xr[s, pl.ds(rows, 2 * rim), c], preferred_element_type=f32
            )
            xr[s, pl.ds(0, rows), c] = grad.astype(bf16)
        gf_out(s).start()
        return carry

    lax.fori_loop(0, slots, late_features, 0)

    def late(t, carry):
        for v in range(U):
            serve(t, v, ORDER)
        return carry

    lax.fori_loop(nch + 2 * slots, nch + (DELAY[-1] + U - 1) // U + 1, late, 0)
    last = local(gb_v.at[5], gb, tsem.at[0])
    last.start()
    last.wait()
    for j in range(5):
        bias_hop(j).wait_send()
    for j in range(2):
        halo_send(j).wait_send()
        back_send(j).wait_send()
        act_out(nch - 2 + j).wait()
    for s in range(slots):
        gf_out(s).wait()
    for k in range(nch - 2, nch):
        for u in range(U):
            c_rs(k, u).wait_send()

    def finish(k, carry):
        for u in range(U):
            for f in (f_rs, a_rs, s_rs, b_rs, s_ag, a_ag, f_ag, c_ag):
                f(k, u).wait_send()
        return carry

    lax.fori_loop(0, nch, finish, 0)


U = 4
Q = 24
DELAY = [4 + 4 * h for h in range(9)]
ORDER = list(range(8, -1, -1))


def main_call(features, weight, bias, cot, seg, offs, marks, edges, edge_marks, rims):
    slots, rows = seg.shape
    total, width = cot.shape
    rim = rims.shape[2]
    nch = width // CH
    half = width // 2
    unit = half // U
    any_ = pl.BlockSpec(memory_space=pl.ANY)
    dma = pltpu.SemaphoreType.DMA
    i32 = jnp.int32
    return pl.pallas_call(
        main_kernel,
        out_shape=(
            jax.ShapeDtypeStruct((total, width), bf16),
            jax.ShapeDtypeStruct((total, width), bf16),
            jax.ShapeDtypeStruct((2 * nch, width, H), bf16),
            jax.ShapeDtypeStruct((nch, CH), f32),
        ),
        in_specs=[any_] * 10,
        out_specs=[any_] * 4,
        scratch_shapes=[
            pltpu.VMEM((slots, rows + 2 * rim, width), bf16),
            pltpu.VMEM((slots, rows + 2 * rim, rows), bf16),
            pltpu.VMEM((slots, rows, 2 * rim), bf16),
            pltpu.VMEM((total, 1), f32),
            pltpu.VMEM((total, width), bf16),
            pltpu.VMEM((width, width), bf16),
            pltpu.VMEM((nch, CH), f32),
            pltpu.VMEM((2, total, CH), bf16),
            pltpu.VMEM((2, total, CH), bf16),
            pltpu.VMEM((total, width), bf16),
            pltpu.VMEM(seg.shape, i32),
            pltpu.VMEM(offs.shape, i32),
            pltpu.VMEM(marks.shape, i32),
            pltpu.VMEM(edges.shape, i32),
            pltpu.VMEM(edge_marks.shape, i32),
            pltpu.VMEM(rims.shape, i32),
            pltpu.VMEM((offs.shape[2], rows), i32),
            pltpu.VMEM((offs.shape[2], rows), i32),
            pltpu.VMEM((4, rim, width), bf16),
            pltpu.VMEM((2, rim, width), bf16),
            pltpu.VMEM((2, 2, half, H), bf16),
            pltpu.VMEM((nch, 2, half, H), bf16),
            pltpu.VMEM((nch, 2, half, H), bf16),
            pltpu.VMEM((nch, U, unit, H), bf16),
            pltpu.VMEM((nch, U, unit // 2, H), bf16),
            pltpu.VMEM((nch, U, unit // 4, H), bf16),
            pltpu.VMEM((nch, U, unit // 4, H), bf16),
            pltpu.VMEM((6, nch, CH), f32),
            pltpu.VMEM((5, nch, CH), f32),
            dma((slots,)),
            dma((7,)),
            dma((nch,)),
            dma((2,)),
            dma((2,)),
            dma((slots,)),
            dma((nch, U)),
            dma((nch, 9 * U)),
            dma((nch, 9 * U)),
            dma((5,)),
            dma((5,)),
            dma((4,)),
            dma((4,)),
        ],
        compiler_params=pltpu.CompilerParams(
            collective_id=0, has_side_effects=True, vmem_limit_bytes=62 << 20
        ),
        name="layer",
    )(features, weight, bias.reshape(nch, CH), cot, seg, offs, marks, edges, edge_marks, rims)


def widen_kernel(ag, out):
    for j in range(ag.shape[0]):
        out[:, j * H : (j + 1) * H] = ag[j].astype(f32)


def widen(ag):
    n, width, _ = ag.shape
    step = 256
    return pl.pallas_call(
        widen_kernel,
        out_shape=jax.ShapeDtypeStruct((width, n * H), f32),
        grid=(width // step,),
        in_specs=[pl.BlockSpec((n, step, H), lambda i: (0, i, 0))],
        out_specs=pl.BlockSpec((step, n * H), lambda i: (i, 0)),
        name="widen",
    )(ag)


def passed_along(value, axis, steps):
    count = lax.axis_size(axis)
    pairs = [(source, (source + steps) % count) for source in range(count)]
    return lax.ppermute(value, axis, pairs)


def tables(seg, offsets, marks, edges, edge_marks, rim):
    slots, rows = seg.shape
    order = jnp.arange(rows, dtype=jnp.int32)
    same = seg[:, :, None] == seg[:, None, :]
    start = jnp.min(jnp.where(same, order, rows), axis=2)
    extent = jnp.sum(same.astype(jnp.int32), axis=2)
    picks = jnp.where(marks == 1, offsets % extent[:, :, None], -1)
    lanes = jnp.arange(128, dtype=jnp.int32)
    near = jnp.sum((picks[:, :, :, None] == lanes).astype(f32), axis=2).astype(bf16)
    spread = (lanes[None, :, None] == (order - start)[:, None, :]).astype(bf16)
    local = jnp.einsum("sio,soj->sij", near, spread, preferred_element_type=f32)
    local = jnp.where(same, local, 0.0) + 2.0 * (order[:, None] == order[None, :])
    joined = jnp.concatenate([edges[:, 0], edges[:, 1] + rim], axis=2)
    joined_marks = jnp.concatenate([edge_marks[:, 0], edge_marks[:, 1]], axis=2)
    cols = jnp.arange(2 * rim, dtype=jnp.int32)
    far = jnp.sum(jnp.where(joined[..., None] == cols, joined_marks[..., None], 0), axis=2)
    degree = jnp.sum(marks, axis=2) + jnp.sum(joined_marks, axis=2)
    return local.astype(bf16), far.astype(bf16), 1.0 / (1.0 + degree.astype(f32))


def spread_out(
    features,
    weight,
    bias,
    cotangent,
    segment_ids,
    neighbour_offsets,
    neighbour_mask,
    halo_edges,
    halo_mask,
    boundary_rows,
):
    slots, rows, width = features.shape
    rim = boundary_rows.shape[2]
    local_counts, halo_counts, scale = tables(
        segment_ids, neighbour_offsets, neighbour_mask, halo_edges, halo_mask, rim
    )
    chosen = (boundary_rows[..., None] == jnp.arange(rows, dtype=jnp.int32)).astype(bf16)
    sent = jnp.einsum("sjbr,srf->sjbf", chosen, features, preferred_element_type=f32).astype(bf16)
    from_prev = passed_along(sent[slots - 1, 1], "blk", 1)
    from_next = passed_along(sent[0, 0], "blk", -1)
    before = jnp.concatenate([from_prev[None], sent[: slots - 1, 1]], axis=0)
    after = jnp.concatenate([sent[1:, 0], from_next[None]], axis=0)
    received = jnp.concatenate([before, after], axis=1)
    summed = jnp.einsum("srk,skf->srf", local_counts, features, preferred_element_type=f32)
    summed = summed + jnp.einsum("srk,skf->srf", halo_counts, received, preferred_element_type=f32)
    mixed = (scale[:, :, None] * summed).astype(bf16).reshape(slots * rows, width)
    incoming = cotangent.reshape(slots * rows, width)
    pre = jnp.dot(mixed, weight, preferred_element_type=f32) + bias[None, :]
    sigma = jax.nn.sigmoid(pre)
    activations = (pre * sigma).astype(bf16)
    grad_pre = (incoming.astype(f32) * (sigma * (1.0 + pre * (1.0 - sigma)))).astype(bf16)
    bias_term = jnp.sum(grad_pre, axis=0, dtype=f32)
    weight_term = lax.dot_general(
        mixed, grad_pre, (((0,), (0,)), ((), ())), preferred_element_type=f32
    )
    grad_weight, grad_bias = lax.psum((weight_term, bias_term), "blk")
    grad_mixed = lax.dot_general(
        grad_pre, weight, (((1,), (1,)), ((), ())), preferred_element_type=f32
    )
    grad_summed = (scale.reshape(-1)[:, None] * grad_mixed).astype(bf16)
    grad_summed = grad_summed.reshape(slots, rows, width)
    grad_received = jnp.einsum(
        "srk,srf->skf", halo_counts, grad_summed, preferred_element_type=f32
    ).astype(bf16)
    toward_prev = grad_received[:, :rim]
    toward_next = grad_received[:, rim:]
    back_prev = passed_along(toward_next[slots - 1], "blk", 1)
    back_next = passed_along(toward_prev[0], "blk", -1)
    grad_first = jnp.concatenate([back_prev[None], toward_next[: slots - 1]], axis=0)
    grad_second = jnp.concatenate([toward_prev[1:], back_next[None]], axis=0)
    grad_sent = jnp.stack([grad_first, grad_second], axis=1)
    grad_features = jnp.einsum(
        "srk,srf->skf", local_counts, grad_summed, preferred_element_type=f32
    ) + jnp.einsum("sjbr,sjbf->srf", chosen, grad_sent, preferred_element_type=f32)
    return (
        activations.reshape(slots, rows, width),
        grad_features.astype(bf16),
        grad_weight,
        grad_bias,
    )


def per_device(
    features,
    weight,
    bias,
    cotangent,
    segment_ids,
    neighbour_offsets,
    neighbour_mask,
    halo_edges,
    halo_mask,
    boundary_rows,
):
    operands = (
        segment_ids,
        neighbour_offsets,
        neighbour_mask,
        halo_edges,
        halo_mask,
        boundary_rows,
    )
    if lax.axis_size("blk") != 32:
        return spread_out(features, weight, bias, cotangent, *operands)
    slots, rows, width = features.shape
    flat = (slots * rows, width)
    activations, grad_features, gathered, grad_bias = main_call(
        features.reshape(flat), weight, bias, cotangent.reshape(flat), *operands
    )
    return (
        activations.reshape(features.shape),
        grad_features.reshape(features.shape),
        widen(gathered),
        grad_bias.reshape(-1),
    )


def solution(mesh):
    in_specs = (
        P("blk", None, None),
        P(),
        P(),
        P("blk", None, None),
        P("blk", None),
        P("blk", None, None),
        P("blk", None, None),
        P("blk", None, None, None),
        P("blk", None, None, None),
        P("blk", None, None),
    )
    out_specs = (P("blk", None, None), P("blk", None, None), P(), P())
    return jax.shard_map(
        per_device, mesh=mesh, in_specs=in_specs, out_specs=out_specs, check_vma=False
    )
```

time: 216 us -> 148 us (0.69)
  matrix products: 47.3 us -> 0 us
  other arithmetic: 33 us -> 0 us
  Pallas kernels: 113 us -> 126 us
  starting transfers between devices: 11.9 us -> 0 us
  local copies, waits for them, and re-layouts: 9 us -> 20.5 us
    dot_general x8 -> x0, matrix products: 47.3 us -> none  [the longest x1 16.3 us: per_device(): lax.dot_general(grad_pre, weight, (((1,), (1,)), ((), ())), preferred_ele...]
    reduce_sum x5 -> x0, other arithmetic: 29.8 us -> none  [the longest x1 15.8 us: tables(): jnp.sum((picks[:, :, :, None] == lanes).astype(f32), axis=2).astype(bf16)]
    unnamed x30 -> x9, local copies, waits for them, and re-layouts: 4.04 us -> 19.2 us
    pallas_call x1, Pallas kernels: 103 us -> 115 us  [main_call(): pl.pallas_call(main_kernel, out_shape=(jax.ShapeDtypeStruct((total, width...]
    ppermute x4 -> x0, starting transfers between devices: 11.9 us -> none  [passed_along(): return lax.ppermute(value, axis, pairs)]
  transfers between devices with their start and end apart: 4 -> 0, of which waited for: 0 -> 0; matrix products, arithmetic and copies ran while one was open for 21% -> 0% of each run, Pallas kernels for 5% -> 0%
where the time goes in v2:
time: 148 us; the launch traced here: 147 us
  Pallas kernels  126 us (85%)
  local copies, waits for them, and re-layouts  20.5 us (14%)
    pallas_call x1, Pallas kernels, main_call(): pl.pallas_call(main_kernel, out_shape=(jax.ShapeDtypeStruct((total, width...  115 us
    unnamed x9, local copies, waits for them, and re-layouts  19.2 us
    pallas_call x1, Pallas kernels, widen(): pl.pallas_call(widen_kernel, out_shape=jax.ShapeDtypeStruct((width, n * H...  10.7 us

profile of v2, /device:TPU:0, one launch (start us, length us, event | category | flops | bytes accessed | tf_op | source)
XLA Modules:
  0.0 147.0 jit_solution(5853478151742118565)
XLA Ops:
  0.6 1.3 reshape.27.bias
  1.9 2.1 %copy.14.offs = s32[4,352,64]{2,1,0:T(8,128)} copy(s32[4,352,64]{1,2,0:T(8,128)} %param.15) | data formatting | bytes 720896 | tf_op args[5]
  4.0 2.1 %copy.15.marks = s32[4,352,64]{2,1,0:T(8,128)} copy(s32[4,352,64]{1,2,0:T(8,128)} %param.16) | data formatting | bytes 720896 | tf_op args[6]
  6.2 2.4 %copy.16.edges = s32[4,2,352,8]{3,2,1,0:T(8,128)} copy(s32[4,2,352,8]{2,3,1,0:T(8,128)} %param.17) | data formatting | bytes 180224 | tf_op args[7]
  8.6 2.4 %copy.17.edge_marks = s32[4,2,352,8]{3,2,1,0:T(8,128)} copy(s32[4,2,352,8]{2,3,1,0:T(8,128)} %param.18) | data formatting | bytes 180224 | tf_op args[8]
  11.0 115.1 %layer.1 = (bf16[1408,2048]{1,0:T(8,128)(2,1)}, bf16[1408,2048]{1,0:T(8,128)(2,1)}, bf16[16,2048,128]{2,1,0:T(8,128)(2,1)}, f32[8,256]{1,0:T(8,128)}) custom-call(bf16[1408,2048]{1,0:T(8,128)(2,1)} %bitcast.8, bf16[2048,2048]{1,0:T(8,128)(2,1)} %w.1, f32[8,256]{1,0:T(8,128)} %reshape.27.bias, bf16[1408,2048]{1,0:T(8,128)(2,1)} %bitcast.9, s32[4,352]{1,0:T(4,128)} %seg.1, ...), custom_call_target="tpu_custom_call" | custom-call | tf_op jit(solution)/shard_map/layer/pallas_call | solution.py:520
  126.1 1.3 copy.18
  127.4 10.7 %widen.1 = f32[2048,2048]{1,0:T(8,128)} custom-call(bf16[16,2048,128]{2,1,0:T(8,128)(2,1)} %get-tuple-element.10.ag), custom_call_target="tpu_custom_call" | custom-call | tf_op jit(solution)/shard_map/widen/pallas_call | solution.py:589
  138.2 0.0 copy-start
  138.2 6.3 %copy.21 = bf16[4,352,2048]{2,1,0:T(8,128)(2,1)} copy(bf16[4,352,2048]{2,1,0:T(8,128)(2,1)} %bitcast.7) | data formatting | bytes 11534336
  144.5 0.0 copy-done
  144.5 2.5 %copy.22 = bf16[4,352,2048]{2,1,0:T(8,128)(2,1)} copy(bf16[4,352,2048]{2,1,0:T(8,128)(2,1)S(1)} %bitcast.6) | data formatting | bytes 11534336
Async XLA Ops:
  138.2 6.3 %copy-start = (bf16[1408,2048]{1,0:T(8,128)(2,1)S(1)}, bf16[1408,2048]{1,0:T(8,128)(2,1)}, u32[]{:S(2)}) copy-start(bf16[1408,2048]{1,0:T(8,128)(2,1)} %get-tuple-element.9) | copy-start | bytes 17301508

commit v3 on v2

--- a/solution.py
+++ b/solution.py
@@ -22,19 +22,19 @@
 
 def main_kernel(
     x, w, bias, cot, seg, offs, marks, edges, edge_marks, rims,
-    act, gf, ag, gb,
-    xr, kt, ot, sc, mixed_v, w_v, bias_v, cot_v, act_v, gp_v,
+    act, xr, ag, gb,
+    kt, ot, sc, mixed_v, w_v, bias_v, cot_v, gp_v,
     seg_v, offs_v, marks_v, edges_v, emarks_v, rims_v, qv, vv, hs, hr,
-    snd, rc, acc, rf, ra, rs, rb, gb_v, gr,
-    xsem, tsem, wsem, csem, asem, fsem, ksem, ssem, rsem, bsem, brsem, hsem, hrsem,
+    snd, rc, fb, rf, ab, ra, sb, rs, rb, gb_v, gr,
+    xsem, tsem, wsem, csem, ssem, rsem, bsem, brsem, hsem, hrsem,
 ):
     n = lax.axis_size("blk")
     me = lax.axis_index("blk")
     slots, deep, width = xr.shape
     rows = kt.shape[2]
     rim = rims_v.shape[2]
-    near = offs_v.shape[2]
-    halo = edges_v.shape[3]
+    near = offs_v.shape[1]
+    halo = edges_v.shape[2]
     total = slots * rows
     nch = width // CH
     half = width // 2
@@ -68,12 +68,6 @@
 
     def cot_in(k):
         return local(cot.at[:, cols(k)], cot_v.at[k % 2], csem.at[k % 2])
-
-    def act_out(k):
-        return local(act_v.at[k % 2], act.at[:, cols(k)], asem.at[k % 2])
-
-    def gf_out(s):
-        return local(xr.at[s, pl.ds(0, rows)], gf.at[slot_rows(s)], fsem.at[s])
 
     small = [
         local(src, dst, tsem.at[i])
@@ -145,17 +139,6 @@
         xr[s - 1, pl.ds(rows + rim, rim), :] = out[:rim]
         xr[s + 1, pl.ds(rows, rim), :] = out[rim:]
 
-    def eye(size):
-        r = lax.broadcasted_iota(jnp.int32, (size, size), 0)
-        c = lax.broadcasted_iota(jnp.int32, (size, size), 1)
-        return jnp.where(r == c, 1.0, 0.0).astype(bf16)
-
-    def turned(value):
-        dims = (((1,), (1,)), ((), ()))
-        return lax.dot_general(
-            eye(value.shape[1]), value.astype(bf16), dims, preferred_element_type=f32
-        ).astype(jnp.int32)
-
     def tables(s, carry):
         seg_r = seg_v[pl.ds(s, 1), :].astype(f32)
         ri = lax.broadcasted_iota(jnp.int32, (rows, rows), 0)
@@ -164,13 +147,13 @@
         seg_c = jnp.sum(jnp.where(diag, seg_r, 0.0), axis=1, keepdims=True)
         start = jnp.sum(jnp.where(seg_r < seg_c, 1.0, 0.0), axis=1, keepdims=True)
         same = seg_r == seg_c
-        size = jnp.sum(jnp.where(same, 1.0, 0.0), axis=1, keepdims=True)
+        size = jnp.sum(jnp.where(same, 1.0, 0.0), axis=0, keepdims=True)
         off = offs_v[s].astype(f32)
         rest = off - jnp.floor((off + 0.5) * (1.0 / size)) * size
         rest = jnp.where(rest < 0.0, rest + size, rest)
         rest = jnp.where(rest >= size, rest - size, rest)
         marked = marks_v[s]
-        pick = turned(jnp.where(marked == 1, rest, 200.0))
+        pick = jnp.where(marked == 1, rest.astype(jnp.int32), 200)
         qv[...] = pick >> 2
         vv[...] = 1 << ((pick & 3) << 3)
         q = lax.broadcasted_iota(jnp.int32, (Q, rows), 0)
@@ -187,16 +170,17 @@
         around = jnp.dot(spread, counts, preferred_element_type=f32)
         around = jnp.where(same, around, 0.0) + jnp.where(diag, 2.0, 0.0)
         kt[s, pl.ds(0, rows), :] = around.astype(bf16)
-        degree = jnp.sum(marked.astype(f32), axis=1, keepdims=True)
+        degree = jnp.sum(marked, axis=0, keepdims=True)
         r = lax.broadcasted_iota(jnp.int32, (rim, rows), 0)
         for j in range(2):
             hot = emarks_v[s, j]
-            degree = degree + jnp.sum(hot.astype(f32), axis=1, keepdims=True)
-            pick = turned(jnp.where(hot == 1, edges_v[s, j].astype(f32), 200.0))
+            degree = degree + jnp.sum(hot, axis=0, keepdims=True)
+            pick = jnp.where(hot == 1, edges_v[s, j], 200)
             far = jnp.zeros((rim, rows), f32)
             for k in range(halo):
                 far = far + jnp.where(pick[k : k + 1, :] == r, 1.0, 0.0)
             kt[s, pl.ds(rows + rim * j, rim), :] = far.astype(bf16)
+        degree = jnp.sum(jnp.where(diag, degree.astype(f32), 0.0), axis=1, keepdims=True)
         sc[slot_rows(s), :] = 1.0 / (1.0 + degree)
         return carry
 
@@ -234,69 +218,84 @@
             r = r + size * b
         return pl.ds(pl.multiple_of(r, 16), size)
 
+    def part(k, j, u, level, flip=False):
+        return ag.at[2 * k + j, at(u, level, flip, half * core)]
+
     def c_rs(k, u):
-        return remote(snd.at[k % 2, :, at(u, 0)], rc.at[k, :, at(u, 0)], k, u, pc)
+        return remote(snd.at[k % 2, :, at(u, 0)], rc.at[k % 4, :, at(u, 0)], k, u, pc)
 
     def f_rs(k, u):
+        return remote(fb.at[k % 2, u], rf.at[k, u], k, U + u, first[u % 2])
+
+    def a_rs(k, u):
+        return remote(ab.at[k % 2, u], ra.at[k, u], k, 2 * U + u, pz1)
+
+    def s_rs(k, u):
+        return remote(sb.at[k % 2, u], rs.at[k, u], k, 3 * U + u, second[u % 2])
+
+    def b_rs(k, u):
+        return remote(part(k, fbit[u % 2], u, 2), rb.at[k, u], k, 4 * U + u, pz2)
+
+    def s_ag(k, u):
+        p = part(k, fbit[u % 2], u, 2)
+        return remote(p, p, k, 5 * U + u, second[u % 2])
+
+    def a_ag(k, u):
+        p = part(k, fbit[u % 2], u, 1)
+        return remote(p, p, k, 6 * U + u, pz1)
+
+    def f_ag(k, u):
+        p = part(k, fbit[u % 2], u, 0)
+        return remote(p, p, k, 7 * U + u, first[u % 2])
+
+    def c_ag(k, u):
+        p = ag.at[pl.ds(2 * k, 2), at(u, 0, False, half * core)]
+        return remote(p, p, k, 8 * U + u, pc)
+
+    def free(send, k, u):
+        @pl.when(k >= 2)
+        def _():
+            send(k - 2, u).wait_send()
+
+    def fold_core(k, u):
         f = fbit[u % 2]
-        return remote(acc.at[k, 1 - f, at(u, 0)], rf.at[k, u], k, U + u, first[u % 2])
-
-    def a_rs(k, u):
-        return remote(acc.at[k, fbit[u % 2], at(u, 1, True)], ra.at[k, u], k, 2 * U + u, pz1)
-
-    def s_rs(k, u):
-        f = fbit[u % 2]
-        return remote(acc.at[k, f, at(u, 2, True)], rs.at[k, u], k, 3 * U + u, second[u % 2])
-
-    def b_rs(k, u):
-        return remote(acc.at[k, fbit[u % 2], at(u, 2)], rb.at[k, u], k, 4 * U + u, pz2)
-
-    def ag_at(k, u, level):
-        return ag.at[2 * k + fbit[u % 2], at(u, level, False, half * core)]
-
-    def keep(k, u):
-        return local(rs.at[k, u], ag_at(k, u, 2), ksem.at[k, u])
-
-    def s_ag(k, u):
-        return remote(rs.at[k, u], ag_at(k, u, 2), k, 5 * U + u, second[u % 2])
-
-    def a_ag(k, u):
-        return remote(ag_at(k, u, 1), ag_at(k, u, 1), k, 6 * U + u, pz1)
-
-    def f_ag(k, u):
-        return remote(ag_at(k, u, 0), ag_at(k, u, 0), k, 7 * U + u, first[u % 2])
-
-    def c_ag(k, u):
-        part = ag.at[pl.ds(2 * k, 2), at(u, 0, False, half * core)]
-        return remote(part, part, k, 8 * U + u, pc)
-
-    def fold(level, buf):
+        free(f_rs, k, u)
+        fb[k % 2, u] = part(k, 1 - f, u, 0)[...] + rc[k % 4, 1 - f, at(u, 0)]
+        p = part(k, f, u, 0)
+        p[...] = p[...] + rc[k % 4, f, at(u, 0)]
+
+    def fold(level, buf, out, send, pick):
         def run(k, u):
             f = fbit[u % 2]
-            d = at(u, level)
-            acc[k, f, d] = acc[k, f, d] + buf[k, u]
+            bit = pick(u)
+            size = (unit >> level) // 2
+            free(send, k, u)
+            away = pl.ds(pl.multiple_of(size * (1 - bit), 16), size)
+            stay = pl.ds(pl.multiple_of(size * bit, 16), size)
+            out[k % 2, u] = part(k, f, u, level + 1, True)[...] + buf[k, u, away]
+            p = part(k, f, u, level + 1)
+            p[...] = p[...] + buf[k, u, stay]
 
         return run
 
-    def fold_core(k, u):
-        d = at(u, 0)
-        for j in range(2):
-            acc[k, j, d] = acc[k, j, d] + rc[k, j, d]
+    def whole(buf):
+        def run(k, u):
+            p = part(k, fbit[u % 2], u, 2)
+            p[...] = p[...] + buf[k, u]
+
+        return run
 
     def last_fold(k, u):
-        rs[k, u] = acc[k, fbit[u % 2], at(u, 2)] + rb[k, u]
-        keep(k, u).start()
-
-    def settle(k, u):
-        keep(k, u).wait()
+        b_rs(k, u).wait_send()
+        whole(rb)(k, u)
 
     hops = [
         (c_rs, fold_core, f_rs),
-        (f_rs, fold(0, rf), a_rs),
-        (a_rs, fold(1, ra), s_rs),
-        (s_rs, fold(2, rs), b_rs),
+        (f_rs, fold(0, rf, ab, a_rs, lambda u: bz1), a_rs),
+        (a_rs, fold(1, ra, sb, s_rs, lambda u: sbit[u % 2]), s_rs),
+        (s_rs, whole(rs), b_rs),
         (b_rs, last_fold, s_ag),
-        (s_ag, settle, a_ag),
+        (s_ag, None, a_ag),
         (a_ag, None, f_ag),
         (f_ag, None, c_ag),
         (c_ag, None, None),
@@ -320,17 +319,17 @@
     def pre_part(k, m):
         mt = total // 2
         d = pl.ds(m * mt, mt)
-        b = bias_v[pl.ds(k, 1), :]
+        b = bias_v[:, cols(k)]
         pre = jnp.dot(mixed_v[d, :], w_v[:, cols(k)], preferred_element_type=f32) + b
         sig = 0.5 * jnp.tanh(0.5 * pre) + 0.5
         out = pre * sig
-        act_v[k % 2, d, :] = out.astype(bf16)
+        act[d, cols(k)] = out.astype(bf16)
         g = (cot_v[k % 2, d, :].astype(f32) * (sig + out * (1.0 - sig))).astype(bf16)
         gp_v[d, cols(k)] = g
         sums = jnp.sum(g.astype(f32), axis=0, keepdims=True)
         if m:
-            sums = sums + gb_v[0, pl.ds(k, 1), :]
-        gb_v[0, pl.ds(k, 1), :] = sums
+            sums = sums + gb_v[0, :, cols(k)]
+        gb_v[0, :, cols(k)] = sums
 
     def grad_part(k, side):
         start = pl.multiple_of(half * side, half)
@@ -340,14 +339,15 @@
         )
 
     def there(k):
-        part = grad_part(k, 1 - core)
-        snd[k % 2, 0] = part[:, :H].astype(bf16)
-        snd[k % 2, 1] = part[:, H:].astype(bf16)
+        grad = grad_part(k, 1 - core)
+        snd[k % 2, 0] = grad[:, :H].astype(bf16)
+        snd[k % 2, 1] = grad[:, H:].astype(bf16)
 
     def here(k):
-        part = grad_part(k, core)
-        acc[k, 0] = part[:, :H].astype(bf16)
-        acc[k, 1] = part[:, H:].astype(bf16)
+        grad = grad_part(k, core)
+        own = pl.ds(pl.multiple_of(half * core, half), half)
+        ag[2 * k, own] = grad[:, :H].astype(bf16)
+        ag[2 * k + 1, own] = grad[:, H:].astype(bf16)
 
     def early(t, more):
         serve(t, 0, ORDER)
@@ -361,10 +361,6 @@
         if more:
             w_in(t + 1).wait()
             cot_in(t + 1).wait()
-
-            @pl.when(t >= 1)
-            def _():
-                act_out(t - 1).wait()
 
         there(t)
         if more:
@@ -376,7 +372,6 @@
         here(t)
         if more:
             pre_part(t + 1, 1)
-            act_out(t + 1).start()
 
             @pl.when(t + 2 < nch)
             def _():
@@ -386,7 +381,6 @@
     cot_in(0).wait()
     pre_part(0, 0)
     pre_part(0, 1)
-    act_out(0).start()
 
     def early_step(t, carry):
         early(t, True)
@@ -466,7 +460,6 @@
                 ot[s], xr[s, pl.ds(rows, 2 * rim), c], preferred_element_type=f32
             )
             xr[s, pl.ds(0, rows), c] = grad.astype(bf16)
-        gf_out(s).start()
         return carry
 
     lax.fori_loop(0, slots, late_features, 0)
@@ -477,24 +470,20 @@
         return carry
 
     lax.fori_loop(nch + 2 * slots, nch + (DELAY[-1] + U - 1) // U + 1, late, 0)
-    last = local(gb_v.at[5], gb, tsem.at[0])
-    last.start()
-    last.wait()
+    gb[...] = gb_v[5]
     for j in range(5):
         bias_hop(j).wait_send()
     for j in range(2):
         halo_send(j).wait_send()
         back_send(j).wait_send()
-        act_out(nch - 2 + j).wait()
-    for s in range(slots):
-        gf_out(s).wait()
     for k in range(nch - 2, nch):
         for u in range(U):
-            c_rs(k, u).wait_send()
+            for f in (c_rs, f_rs, a_rs, s_rs):
+                f(k, u).wait_send()
 
     def finish(k, carry):
         for u in range(U):
-            for f in (f_rs, a_rs, s_rs, b_rs, s_ag, a_ag, f_ag, c_ag):
+            for f in (s_ag, a_ag, f_ag, c_ag):
                 f(k, u).wait_send()
         return carry
 
@@ -520,22 +509,20 @@
     return pl.pallas_call(
         main_kernel,
         out_shape=(
-            jax.ShapeDtypeStruct((total, width), bf16),
-            jax.ShapeDtypeStruct((total, width), bf16),
-            jax.ShapeDtypeStruct((2 * nch, width, H), bf16),
-            jax.ShapeDtypeStruct((nch, CH), f32),
+            pltpu.VMEM((total, width), bf16),
+            pltpu.VMEM((slots, rows + 2 * rim, width), bf16),
+            pltpu.VMEM((2 * nch, width, H), bf16),
+            pltpu.VMEM((1, width), f32),
         ),
         in_specs=[any_] * 10,
-        out_specs=[any_] * 4,
+        out_specs=[pl.BlockSpec(memory_space=pltpu.VMEM)] * 4,
         scratch_shapes=[
-            pltpu.VMEM((slots, rows + 2 * rim, width), bf16),
             pltpu.VMEM((slots, rows + 2 * rim, rows), bf16),
             pltpu.VMEM((slots, rows, 2 * rim), bf16),
             pltpu.VMEM((total, 1), f32),
             pltpu.VMEM((total, width), bf16),
             pltpu.VMEM((width, width), bf16),
-            pltpu.VMEM((nch, CH), f32),
-            pltpu.VMEM((2, total, CH), bf16),
+            pltpu.VMEM((1, width), f32),
             pltpu.VMEM((2, total, CH), bf16),
             pltpu.VMEM((total, width), bf16),
             pltpu.VMEM(seg.shape, i32),
@@ -544,26 +531,25 @@
             pltpu.VMEM(edges.shape, i32),
             pltpu.VMEM(edge_marks.shape, i32),
             pltpu.VMEM(rims.shape, i32),
-            pltpu.VMEM((offs.shape[2], rows), i32),
-            pltpu.VMEM((offs.shape[2], rows), i32),
+            pltpu.VMEM((offs.shape[1], rows), i32),
+            pltpu.VMEM((offs.shape[1], rows), i32),
             pltpu.VMEM((4, rim, width), bf16),
             pltpu.VMEM((2, rim, width), bf16),
             pltpu.VMEM((2, 2, half, H), bf16),
-            pltpu.VMEM((nch, 2, half, H), bf16),
-            pltpu.VMEM((nch, 2, half, H), bf16),
+            pltpu.VMEM((4, 2, half, H), bf16),
+            pltpu.VMEM((2, U, unit, H), bf16),
             pltpu.VMEM((nch, U, unit, H), bf16),
+            pltpu.VMEM((2, U, unit // 2, H), bf16),
             pltpu.VMEM((nch, U, unit // 2, H), bf16),
+            pltpu.VMEM((2, U, unit // 4, H), bf16),
             pltpu.VMEM((nch, U, unit // 4, H), bf16),
             pltpu.VMEM((nch, U, unit // 4, H), bf16),
-            pltpu.VMEM((6, nch, CH), f32),
-            pltpu.VMEM((5, nch, CH), f32),
+            pltpu.VMEM((6, 1, width), f32),
+            pltpu.VMEM((5, 1, width), f32),
             dma((slots,)),
             dma((7,)),
             dma((nch,)),
             dma((2,)),
-            dma((2,)),
-            dma((slots,)),
-            dma((nch, U)),
             dma((nch, 9 * U)),
             dma((nch, 9 * U)),
             dma((5,)),
@@ -572,28 +558,62 @@
             dma((4,)),
         ],
         compiler_params=pltpu.CompilerParams(
-            collective_id=0, has_side_effects=True, vmem_limit_bytes=62 << 20
+            collective_id=0, has_side_effects=True, vmem_limit_bytes=40 << 20
         ),
         name="layer",
-    )(features, weight, bias.reshape(nch, CH), cot, seg, offs, marks, edges, edge_marks, rims)
-
-
-def widen_kernel(ag, out):
-    for j in range(ag.shape[0]):
-        out[:, j * H : (j + 1) * H] = ag[j].astype(f32)
-
-
-def widen(ag):
-    n, width, _ = ag.shape
-    step = 256
+    )(features, weight, bias, cot, seg, offs, marks, edges, edge_marks, rims)
+
+
+def finish_kernel(act, xr, ag, gb, act_o, gf_o, gw_o, gb_o, stage, sem, ssem):
+    slots, rows, _ = gf_o.shape
+    step = stage.shape[1]
+    plain = [(gb, gb_o), (act, act_o)]
+    plain += [(xr.at[s, pl.ds(0, rows)], gf_o.at[s]) for s in range(slots)]
+    plain = [pltpu.make_async_copy(a, b, sem.at[i]) for i, (a, b) in enumerate(plain)]
+
+    def out(i):
+        return pltpu.make_async_copy(
+            stage.at[i % 2], gw_o.at[pl.ds(i * step, step)], ssem.at[i % 2]
+        )
+
+    steps = gw_o.shape[0] // step
+    for i in range(steps):
+        if i >= 2:
+            out(i - 2).wait()
+        for j in range(ag.shape[0]):
+            stage[i % 2, :, j * H : (j + 1) * H] = ag[j, i * step : (i + 1) * step].astype(f32)
+        out(i).start()
+        if i == 0:
+            for c in plain:
+                c.start()
+    out(steps - 2).wait()
+    out(steps - 1).wait()
+    for c in plain:
+        c.wait()
+
+
+def finish(act, xr, ag, gb, rows):
+    slots, _, width = xr.shape
+    vmem = pl.BlockSpec(memory_space=pltpu.VMEM)
+    any_ = pl.BlockSpec(memory_space=pl.ANY)
     return pl.pallas_call(
-        widen_kernel,
-        out_shape=jax.ShapeDtypeStruct((width, n * H), f32),
-        grid=(width // step,),
-        in_specs=[pl.BlockSpec((n, step, H), lambda i: (0, i, 0))],
-        out_specs=pl.BlockSpec((step, n * H), lambda i: (i, 0)),
-        name="widen",
-    )(ag)
+        finish_kernel,
+        out_shape=(
+            jax.ShapeDtypeStruct(act.shape, bf16),
+            jax.ShapeDtypeStruct((slots, rows, width), bf16),
+            jax.ShapeDtypeStruct((width, width), f32),
+            jax.ShapeDtypeStruct((1, width), f32),
+        ),
+        in_specs=[vmem] * 4,
+        out_specs=[any_] * 4,
+        scratch_shapes=[
+            pltpu.VMEM((2, 256, width), f32),
+            pltpu.SemaphoreType.DMA((2 + slots,)),
+            pltpu.SemaphoreType.DMA((2,)),
+        ],
+        compiler_params=pltpu.CompilerParams(vmem_limit_bytes=6 << 20),
+        name="finish",
+    )(act, xr, ag, gb)
 
 
 def passed_along(value, axis, steps):
@@ -709,13 +729,23 @@
         return spread_out(features, weight, bias, cotangent, *operands)
     slots, rows, width = features.shape
     flat = (slots * rows, width)
-    activations, grad_features, gathered, grad_bias = main_call(
-        features.reshape(flat), weight, bias, cotangent.reshape(flat), *operands
-    )
+    held = main_call(
+        features.reshape(flat),
+        weight,
+        bias.reshape(1, width),
+        cotangent.reshape(flat),
+        segment_ids,
+        jnp.swapaxes(neighbour_offsets, 1, 2),
+        jnp.swapaxes(neighbour_mask, 1, 2),
+        jnp.swapaxes(halo_edges, 2, 3),
+        jnp.swapaxes(halo_mask, 2, 3),
+        boundary_rows,
+    )
+    activations, grad_features, grad_weight, grad_bias = finish(*held, rows)
     return (
         activations.reshape(features.shape),
-        grad_features.reshape(features.shape),
-        widen(gathered),
+        grad_features,
+        grad_weight,
         grad_bias.reshape(-1),
     )
 

time: 148 us -> 121 us (0.82)
  local copies, waits for them, and re-layouts: 20.5 us -> 0 us
  Pallas kernels: 126 us -> 120 us
    unnamed x9 -> x0, local copies, waits for them, and re-layouts: 19.2 us -> none
    pallas_call x2, Pallas kernels: 126 us -> 120 us  [the longest x1 110 us: main_call(): pl.pallas_call(main_kernel, out_shape=(pltpu.VMEM((total, width), bf16),...]
where the time goes in v3:
time: 121 us
  Pallas kernels  120 us (99%)
    pallas_call x1, Pallas kernels, main_call(): pl.pallas_call(main_kernel, out_shape=(pltpu.VMEM((total, width), bf16),...  110 us
    pallas_call x1, Pallas kernels, finish(): pl.pallas_call(finish_kernel, out_shape=(jax.ShapeDtypeStruct(act.shape,...  10.4 us

profile of v3, /device:TPU:0, one launch (start us, length us, event | category | flops | bytes accessed | tf_op | source)
XLA Modules:
  0.0 120.8 jit_solution(16028402939515427698)
XLA Ops:
  0.6 109.7 %layer.1 = (bf16[1408,2048]{1,0:T(8,128)(2,1)S(1)}, bf16[4,480,2048]{2,1,0:T(8,128)(2,1)S(1)}, bf16[16,2048,128]{2,1,0:T(8,128)(2,1)S(1)}, f32[1,2048]{1,0:T(1,128)S(1)}) custom-call(bf16[1408,2048]{1,0:T(8,128)(2,1)} %bitcast.9, bf16[2048,2048]{1,0:T(8,128)(2,1)} %w.1, f32[1,2048]{1,0:T(1,128)} %bitcast.15, bf16[1408,2048]{1,0:T(8,128)(2,1)} %bitcast.10, ...), custom_call_target="tpu_custom_call" | custom-call | tf_op jit(solution)/shard_map/layer/pallas_call | solution.py:509
  110.3 10.4 %finish.1 = (bf16[1408,2048]{1,0:T(8,128)(2,1)}, bf16[4,352,2048]{2,1,0:T(8,128)(2,1)}, f32[2048,2048]{1,0:T(8,128)}, f32[1,2048]{1,0:T(1,128)}) custom-call(bf16[1408,2048]{1,0:T(8,128)(2,1)S(1)} %get-tuple-element.12.act, bf16[4,480,2048]{2,1,0:T(8,128)(2,1)S(1)} %get-tuple-element.13.xr, bf16[16,2048,128]{2,1,0:T(8,128)(2,1)S(1)} %get-tuple-element.14.ag, ...), custom_call_target="tpu_custom_call" | custom-call | tf_op jit(solution)/shard_map/finish/pallas_call | solution.py:599

commit v4 on v3

--- a/solution.py
+++ b/solution.py
@@ -26,7 +26,7 @@
     kt, ot, sc, mixed_v, w_v, bias_v, cot_v, gp_v,
     seg_v, offs_v, marks_v, edges_v, emarks_v, rims_v, qv, vv, hs, hr,
     snd, rc, fb, rf, ab, ra, sb, rs, rb, gb_v, gr,
-    xsem, tsem, wsem, csem, ssem, rsem, bsem, brsem, hsem, hrsem,
+    xsem, tsem, wsem, csem, ssem, rcsem, rsem, bsem, brsem, hsem, hrsem,
 ):
     n = lax.axis_size("blk")
     me = lax.axis_index("blk")
@@ -90,11 +90,6 @@
         c.start()
     for s in range(1, slots - 1):
         x_in(s).start()
-    w_in(0).start()
-    cot_in(0).start()
-    cot_in(1).start()
-    for k in range(1, nch):
-        w_in(k).start()
 
     def offer(s):
         picks = jnp.concatenate([rims_v[s, 0:1, :], rims_v[s, 1:2, :]], axis=1)
@@ -131,6 +126,11 @@
     pl.semaphore_wait(barrier, 7)
     halo_send(0).start()
     halo_send(1).start()
+    w_in(0).start()
+    cot_in(0).start()
+    for k in range(1, nch):
+        w_in(k).start()
+    cot_in(1).start()
     for c in small[1:]:
         c.wait()
     for s in range(1, slots - 1):
@@ -184,7 +184,7 @@
         sc[slot_rows(s), :] = 1.0 / (1.0 + degree)
         return carry
 
-    lax.fori_loop(0, slots, tables, 0)
+    lax.fori_loop(0, slots, tables, 0, unroll=True)
 
     def mix(s):
         d = slot_rows(s)
@@ -194,16 +194,40 @@
             summed = lax.dot_general(kt[s], xr[s, :, c], dims, preferred_element_type=f32)
             mixed_v[d, c] = (sc[d, :] * summed).astype(bf16)
 
+    def pre_part(k, start, count, more):
+        d = pl.ds(start, count)
+        b = bias_v[:, cols(k)]
+        pre = jnp.dot(mixed_v[d, :], w_v[:, cols(k)], preferred_element_type=f32) + b
+        sig = 0.5 * jnp.tanh(0.5 * pre) + 0.5
+        out = pre * sig
+        act[d, cols(k)] = out.astype(bf16)
+        g = (cot_v[k % 2, d, :].astype(f32) * (sig + out * (1.0 - sig))).astype(bf16)
+        gp_v[d, cols(k)] = g
+        sums = jnp.sum(g.astype(f32), axis=0, keepdims=True)
+        if more:
+            sums = sums + gb_v[0, :, cols(k)]
+        gb_v[0, :, cols(k)] = sums
+
     for s in range(1, slots - 1):
         mix(s)
+    w_in(0).wait()
+    cot_in(0).wait()
+    pre_part(0, rows, total - 2 * rows, False)
     halo_send(0).wait_recv()
     halo_send(1).wait_recv()
     mix(0)
     mix(slots - 1)
+    pre_part(0, 0, rows, True)
+    pre_part(0, total - rows, rows, True)
 
     def remote(src, dst, k, s, to):
         return pltpu.make_async_remote_copy(
-            src, dst, ssem.at[k, s], rsem.at[k, s], device_id=(to,), device_id_type=MESH
+            src,
+            dst,
+            ssem.at[k % 2, s],
+            rsem.at[k % 2, s],
+            device_id=(to,),
+            device_id_type=MESH,
         )
 
     def at(u, level, flip=False, base=0):
@@ -222,7 +246,14 @@
         return ag.at[2 * k + j, at(u, level, flip, half * core)]
 
     def c_rs(k, u):
-        return remote(snd.at[k % 2, :, at(u, 0)], rc.at[k % 4, :, at(u, 0)], k, u, pc)
+        return pltpu.make_async_remote_copy(
+            snd.at[k % 2, :, at(u, 0)],
+            rc.at[k % 4, :, at(u, 0)],
+            ssem.at[k % 2, u],
+            rcsem.at[k % 4, u],
+            device_id=(pc,),
+            device_id_type=MESH,
+        )
 
     def f_rs(k, u):
         return remote(fb.at[k % 2, u], rf.at[k, u], k, U + u, first[u % 2])
@@ -313,23 +344,10 @@
                 took(k, u).wait_recv()
                 if work is not None:
                     work(k, u)
+                if h >= 4 and send is not None:
+                    free(send, k, u)
                 if send is not None:
                     send(k, u).start()
-
-    def pre_part(k, m):
-        mt = total // 2
-        d = pl.ds(m * mt, mt)
-        b = bias_v[:, cols(k)]
-        pre = jnp.dot(mixed_v[d, :], w_v[:, cols(k)], preferred_element_type=f32) + b
-        sig = 0.5 * jnp.tanh(0.5 * pre) + 0.5
-        out = pre * sig
-        act[d, cols(k)] = out.astype(bf16)
-        g = (cot_v[k % 2, d, :].astype(f32) * (sig + out * (1.0 - sig))).astype(bf16)
-        gp_v[d, cols(k)] = g
-        sums = jnp.sum(g.astype(f32), axis=0, keepdims=True)
-        if m:
-            sums = sums + gb_v[0, :, cols(k)]
-        gb_v[0, :, cols(k)] = sums
 
     def grad_part(k, side):
         start = pl.multiple_of(half * side, half)
@@ -364,23 +382,18 @@
 
         there(t)
         if more:
-            pre_part(t + 1, 0)
+            pre_part(t + 1, 0, total // 2, False)
         for u in range(U):
             c_rs(t, u).start()
         serve(t, 2, ORDER)
         serve(t, 3, ORDER)
         here(t)
         if more:
-            pre_part(t + 1, 1)
+            pre_part(t + 1, total // 2, total // 2, True)
 
             @pl.when(t + 2 < nch)
             def _():
                 cot_in(t + 2).start()
-
-    w_in(0).wait()
-    cot_in(0).wait()
-    pre_part(0, 0)
-    pre_part(0, 1)
 
     def early_step(t, carry):
         early(t, True)
@@ -478,16 +491,8 @@
         back_send(j).wait_send()
     for k in range(nch - 2, nch):
         for u in range(U):
-            for f in (c_rs, f_rs, a_rs, s_rs):
+            for f in (c_rs, f_rs, a_rs, s_rs, s_ag, a_ag, f_ag, c_ag):
                 f(k, u).wait_send()
-
-    def finish(k, carry):
-        for u in range(U):
-            for f in (s_ag, a_ag, f_ag, c_ag):
-                f(k, u).wait_send()
-        return carry
-
-    lax.fori_loop(0, nch, finish, 0)
 
 
 U = 4
@@ -550,8 +555,9 @@
             dma((7,)),
             dma((nch,)),
             dma((2,)),
-            dma((nch, 9 * U)),
-            dma((nch, 9 * U)),
+            dma((2, 9 * U)),
+            dma((4, U)),
+            dma((2, 9 * U)),
             dma((5,)),
             dma((5,)),
             dma((4,)),

time: 121 us -> 117 us (0.967)
  Pallas kernels: 120 us -> 115 us
    pallas_call x1, Pallas kernels: 110 us -> 105 us  [main_call(): pl.pallas_call(main_kernel, out_shape=(pltpu.VMEM((total, width), bf16),...]
where the time goes in v4:
time: 117 us; the launch traced here: 116 us
  Pallas kernels  115 us (98%)
    pallas_call x1, Pallas kernels, main_call(): pl.pallas_call(main_kernel, out_shape=(pltpu.VMEM((total, width), bf16),...  105 us
    pallas_call x1, Pallas kernels, finish(): pl.pallas_call(finish_kernel, out_shape=(jax.ShapeDtypeStruct(act.shape,...  10.4 us

profile of v4, /device:TPU:0, one launch (start us, length us, event | category | flops | bytes accessed | tf_op | source)
XLA Modules:
  0.0 116.3 jit_solution(9030332494841512404)
XLA Ops:
  0.6 105.1 %layer.1 = (bf16[1408,2048]{1,0:T(8,128)(2,1)S(1)}, bf16[4,480,2048]{2,1,0:T(8,128)(2,1)S(1)}, bf16[16,2048,128]{2,1,0:T(8,128)(2,1)S(1)}, f32[1,2048]{1,0:T(1,128)S(1)}) custom-call(bf16[1408,2048]{1,0:T(8,128)(2,1)} %bitcast.9, bf16[2048,2048]{1,0:T(8,128)(2,1)} %w.1, f32[1,2048]{1,0:T(1,128)} %bitcast.15, bf16[1408,2048]{1,0:T(8,128)(2,1)} %bitcast.10, ...), custom_call_target="tpu_custom_call" | custom-call | tf_op jit(solution)/shard_map/layer/pallas_call | solution.py:514
  105.7 10.4 %finish.1 = (bf16[1408,2048]{1,0:T(8,128)(2,1)}, bf16[4,352,2048]{2,1,0:T(8,128)(2,1)}, f32[2048,2048]{1,0:T(8,128)}, f32[1,2048]{1,0:T(1,128)}) custom-call(bf16[1408,2048]{1,0:T(8,128)(2,1)S(1)} %get-tuple-element.12.act, bf16[4,480,2048]{2,1,0:T(8,128)(2,1)S(1)} %get-tuple-element.13.xr, bf16[16,2048,128]{2,1,0:T(8,128)(2,1)S(1)} %get-tuple-element.14.ag, ...), custom_call_target="tpu_custom_call" | custom-call | tf_op jit(solution)/shard_map/finish/pallas_call | solution.py:605

commit v5 on v4

--- a/solution.py
+++ b/solution.py
@@ -47,6 +47,11 @@
     second = [first[1], first[0]]
     sbit = [fbit[1], fbit[0]]
 
+    def middle(u):
+        pair = [(bz1, pz1), (sbit[u % 2], second[u % 2])]
+        return pair[::-1] if u in TURNED else pair
+
+
     barrier = pltpu.get_barrier_semaphore()
     for p in (pc, px, py, pz1, pz2, prev, nxt):
         pl.semaphore_signal(barrier, inc=1, device_id=(p,), device_id_type=MESH)
@@ -63,8 +68,9 @@
     def x_in(s):
         return local(x.at[slot_rows(s)], xr.at[s, pl.ds(0, rows)], xsem.at[s])
 
-    def w_in(k):
-        return local(w.at[:, cols(k)], w_v.at[:, cols(k)], wsem.at[k])
+    def w_in(i):
+        c = (pl.ds(0, CH), pl.ds(CH, width - CH))[i]
+        return local(w.at[:, c], w_v.at[:, c], wsem.at[i])
 
     def cot_in(k):
         return local(cot.at[:, cols(k)], cot_v.at[k % 2], csem.at[k % 2])
@@ -100,17 +106,19 @@
             ot[s], xr[s, pl.ds(0, rows), :], dims, preferred_element_type=f32
         ).astype(bf16)
 
-    def halo_send(j):
+    def halo_send(j, q):
         s, to = ((0, nxt), (slots - 1, prev))[j]
-        dst = xr.at[s, pl.ds(rows + rim * j, rim)]
+        c = pl.ds(q * half, half)
+        i = 2 * j + q
         return pltpu.make_async_remote_copy(
-            hs.at[j], dst, hsem.at[j], hrsem.at[j], device_id=(to,), device_id_type=MESH
+            hs.at[j, :, c], xr.at[s, pl.ds(rows + rim * j, rim), c], hsem.at[i], hrsem.at[i],
+            device_id=(to,), device_id_type=MESH,
         )
 
     def back_send(j):
         to = (prev, nxt)[j]
         return pltpu.make_async_remote_copy(
-            hs.at[2 + j], hr.at[j], hsem.at[2 + j], hrsem.at[2 + j],
+            hs.at[2 + j], hr.at[j], hsem.at[4 + j], hrsem.at[4 + j],
             device_id=(to,), device_id_type=MESH,
         )
 
@@ -124,13 +132,13 @@
     hs[0] = out[rim:]
     xr[slots - 2, pl.ds(rows + rim, rim), :] = out[:rim]
     pl.semaphore_wait(barrier, 7)
-    halo_send(0).start()
-    halo_send(1).start()
+    for q in range(2):
+        for j in range(2):
+            halo_send(j, q).start()
     w_in(0).start()
     cot_in(0).start()
-    for k in range(1, nch):
-        w_in(k).start()
     cot_in(1).start()
+    w_in(1).start()
     for c in small[1:]:
         c.wait()
     for s in range(1, slots - 1):
@@ -186,10 +194,10 @@
 
     lax.fori_loop(0, slots, tables, 0, unroll=True)
 
-    def mix(s):
+    def mix(s, tiles):
         d = slot_rows(s)
         dims = (((0,), (0,)), ((), ()))
-        for j in range(4):
+        for j in tiles:
             c = pl.ds(j * (width // 4), width // 4)
             summed = lax.dot_general(kt[s], xr[s, :, c], dims, preferred_element_type=f32)
             mixed_v[d, c] = (sc[d, :] * summed).astype(bf16)
@@ -209,14 +217,15 @@
         gb_v[0, :, cols(k)] = sums
 
     for s in range(1, slots - 1):
-        mix(s)
+        mix(s, range(4))
     w_in(0).wait()
     cot_in(0).wait()
     pre_part(0, rows, total - 2 * rows, False)
-    halo_send(0).wait_recv()
-    halo_send(1).wait_recv()
-    mix(0)
-    mix(slots - 1)
+    for q in range(2):
+        for j in range(2):
+            halo_send(j, q).wait_recv()
+        mix(0, (2 * q, 2 * q + 1))
+        mix(slots - 1, (2 * q, 2 * q + 1))
     pre_part(0, 0, rows, True)
     pre_part(0, total - rows, rows, True)
 
@@ -225,7 +234,7 @@
             src,
             dst,
             ssem.at[k % 2, s],
-            rsem.at[k % 2, s],
+            rsem.at[k % 2, s - U],
             device_id=(to,),
             device_id_type=MESH,
         )
@@ -233,7 +242,7 @@
     def at(u, level, flip=False, base=0):
         r = base + unit * u
         size = unit
-        picks = [bz1, sbit[u % 2]]
+        picks = [bit for bit, _ in middle(u)]
         for j in range(level):
             size = size // 2
             b = picks[j]
@@ -259,21 +268,21 @@
         return remote(fb.at[k % 2, u], rf.at[k, u], k, U + u, first[u % 2])
 
     def a_rs(k, u):
-        return remote(ab.at[k % 2, u], ra.at[k, u], k, 2 * U + u, pz1)
+        return remote(ab.at[k % 2, u], ra.at[k, u], k, 2 * U + u, middle(u)[0][1])
 
     def s_rs(k, u):
-        return remote(sb.at[k % 2, u], rs.at[k, u], k, 3 * U + u, second[u % 2])
+        return remote(sb.at[k % 2, u], rs.at[k, u], k, 3 * U + u, middle(u)[1][1])
 
     def b_rs(k, u):
         return remote(part(k, fbit[u % 2], u, 2), rb.at[k, u], k, 4 * U + u, pz2)
 
     def s_ag(k, u):
         p = part(k, fbit[u % 2], u, 2)
-        return remote(p, p, k, 5 * U + u, second[u % 2])
+        return remote(p, p, k, 5 * U + u, middle(u)[1][1])
 
     def a_ag(k, u):
         p = part(k, fbit[u % 2], u, 1)
-        return remote(p, p, k, 6 * U + u, pz1)
+        return remote(p, p, k, 6 * U + u, middle(u)[0][1])
 
     def f_ag(k, u):
         p = part(k, fbit[u % 2], u, 0)
@@ -295,10 +304,10 @@
         p = part(k, f, u, 0)
         p[...] = p[...] + rc[k % 4, f, at(u, 0)]
 
-    def fold(level, buf, out, send, pick):
+    def fold(level, buf, out, send):
         def run(k, u):
             f = fbit[u % 2]
-            bit = pick(u)
+            bit = middle(u)[level][0]
             size = (unit >> level) // 2
             free(send, k, u)
             away = pl.ds(pl.multiple_of(size * (1 - bit), 16), size)
@@ -322,8 +331,8 @@
 
     hops = [
         (c_rs, fold_core, f_rs),
-        (f_rs, fold(0, rf, ab, a_rs, lambda u: bz1), a_rs),
-        (a_rs, fold(1, ra, sb, s_rs, lambda u: sbit[u % 2]), s_rs),
+        (f_rs, fold(0, rf, ab, a_rs), a_rs),
+        (a_rs, fold(1, ra, sb, s_rs), s_rs),
         (s_rs, whole(rs), b_rs),
         (b_rs, last_fold, s_ag),
         (s_ag, None, a_ag),
@@ -377,8 +386,11 @@
                 c_rs(t - 2, u).wait_send()
 
         if more:
-            w_in(t + 1).wait()
             cot_in(t + 1).wait()
+
+            @pl.when(t == 0)
+            def _():
+                w_in(1).wait()
 
         there(t)
         if more:
@@ -487,7 +499,8 @@
     for j in range(5):
         bias_hop(j).wait_send()
     for j in range(2):
-        halo_send(j).wait_send()
+        for q in range(2):
+            halo_send(j, q).wait_send()
         back_send(j).wait_send()
     for k in range(nch - 2, nch):
         for u in range(U):
@@ -496,6 +509,7 @@
 
 
 U = 4
+TURNED = (0,)
 Q = 24
 DELAY = [4 + 4 * h for h in range(9)]
 ORDER = list(range(8, -1, -1))
@@ -553,15 +567,15 @@
             pltpu.VMEM((5, 1, width), f32),
             dma((slots,)),
             dma((7,)),
-            dma((nch,)),
+            dma((2,)),
             dma((2,)),
             dma((2, 9 * U)),
             dma((4, U)),
-            dma((2, 9 * U)),
+            dma((2, 8 * U)),
             dma((5,)),
             dma((5,)),
-            dma((4,)),
-            dma((4,)),
+            dma((6,)),
+            dma((6,)),
         ],
         compiler_params=pltpu.CompilerParams(
             collective_id=0, has_side_effects=True, vmem_limit_bytes=40 << 20
@@ -572,28 +586,28 @@
 
 def finish_kernel(act, xr, ag, gb, act_o, gf_o, gw_o, gb_o, stage, sem, ssem):
     slots, rows, _ = gf_o.shape
-    step = stage.shape[1]
+    n, step, _ = stage.shape
     plain = [(gb, gb_o), (act, act_o)]
     plain += [(xr.at[s, pl.ds(0, rows)], gf_o.at[s]) for s in range(slots)]
     plain = [pltpu.make_async_copy(a, b, sem.at[i]) for i, (a, b) in enumerate(plain)]
 
     def out(i):
         return pltpu.make_async_copy(
-            stage.at[i % 2], gw_o.at[pl.ds(i * step, step)], ssem.at[i % 2]
+            stage.at[i % n], gw_o.at[pl.ds(i * step, step)], ssem.at[i % n]
         )
 
     steps = gw_o.shape[0] // step
     for i in range(steps):
-        if i >= 2:
-            out(i - 2).wait()
+        if i >= n:
+            out(i - n).wait()
         for j in range(ag.shape[0]):
-            stage[i % 2, :, j * H : (j + 1) * H] = ag[j, i * step : (i + 1) * step].astype(f32)
+            stage[i % n, :, j * H : (j + 1) * H] = ag[j, i * step : (i + 1) * step].astype(f32)
         out(i).start()
         if i == 0:
             for c in plain:
                 c.start()
-    out(steps - 2).wait()
-    out(steps - 1).wait()
+    for i in range(steps - n, steps):
+        out(i).wait()
     for c in plain:
         c.wait()
 
@@ -613,9 +627,9 @@
         in_specs=[vmem] * 4,
         out_specs=[any_] * 4,
         scratch_shapes=[
-            pltpu.VMEM((2, 256, width), f32),
+            pltpu.VMEM((4, 128, width), f32),
             pltpu.SemaphoreType.DMA((2 + slots,)),
-            pltpu.SemaphoreType.DMA((2,)),
+            pltpu.SemaphoreType.DMA((4,)),
         ],
         compiler_params=pltpu.CompilerParams(vmem_limit_bytes=6 << 20),
         name="finish",

time: 117 us -> 115 us (0.983)
  no operation moved by 1% of the time
where the time goes in v5:
time: 115 us
  Pallas kernels  114 us (99%)
    pallas_call x1, Pallas kernels, main_call(): pl.pallas_call(main_kernel, out_shape=(pltpu.VMEM((total, width), bf16),...  105 us
    pallas_call x1, Pallas kernels, finish(): pl.pallas_call(finish_kernel, out_shape=(jax.ShapeDtypeStruct(act.shape,...  9.43 us

profile of v5, /device:TPU:0, one launch (start us, length us, event | category | flops | bytes accessed | tf_op | source)
XLA Modules:
  0.0 115.0 jit_solution(8481064946272093133)
XLA Ops:
  0.6 104.7 %layer.1 = (bf16[1408,2048]{1,0:T(8,128)(2,1)S(1)}, bf16[4,480,2048]{2,1,0:T(8,128)(2,1)S(1)}, bf16[16,2048,128]{2,1,0:T(8,128)(2,1)S(1)}, f32[1,2048]{1,0:T(1,128)S(1)}) custom-call(bf16[1408,2048]{1,0:T(8,128)(2,1)} %bitcast.9, bf16[2048,2048]{1,0:T(8,128)(2,1)} %w.1, f32[1,2048]{1,0:T(1,128)} %bitcast.15, bf16[1408,2048]{1,0:T(8,128)(2,1)} %bitcast.10, ...), custom_call_target="tpu_custom_call" | custom-call | tf_op jit(solution)/shard_map/layer/pallas_call | solution.py:528
  105.4 9.4 %finish.1 = (bf16[1408,2048]{1,0:T(8,128)(2,1)}, bf16[4,352,2048]{2,1,0:T(8,128)(2,1)}, f32[2048,2048]{1,0:T(8,128)}, f32[1,2048]{1,0:T(1,128)}) custom-call(bf16[1408,2048]{1,0:T(8,128)(2,1)S(1)} %get-tuple-element.12.act, bf16[4,480,2048]{2,1,0:T(8,128)(2,1)S(1)} %get-tuple-element.13.xr, bf16[16,2048,128]{2,1,0:T(8,128)(2,1)S(1)} %get-tuple-element.14.ag, ...), custom_call_target="tpu_custom_call" | custom-call | tf_op jit(solution)/shard_map/finish/pallas_call | solution.py:619

commit v6 on v5

--- a/solution.py
+++ b/solution.py
@@ -26,7 +26,7 @@
     kt, ot, sc, mixed_v, w_v, bias_v, cot_v, gp_v,
     seg_v, offs_v, marks_v, edges_v, emarks_v, rims_v, qv, vv, hs, hr,
     snd, rc, fb, rf, ab, ra, sb, rs, rb, gb_v, gr,
-    xsem, tsem, wsem, csem, ssem, rcsem, rsem, bsem, brsem, hsem, hrsem,
+    xsem, tsem, wsem, csem, ssem, rcsem, resem, rsem, bsem, brsem, hsem, hrsem,
 ):
     n = lax.axis_size("blk")
     me = lax.axis_index("blk")
@@ -284,8 +284,19 @@
         p = part(k, fbit[u % 2], u, 1)
         return remote(p, p, k, 6 * U + u, middle(u)[0][1])
 
+    def e_ag(k, u):
+        p = part(k, fbit[u % 2], u, 1)
+        return pltpu.make_async_remote_copy(
+            p,
+            p,
+            ssem.at[k % 2, 9 * U + u],
+            resem.at[k % 4, u],
+            device_id=(first[u % 2],),
+            device_id_type=MESH,
+        )
+
     def f_ag(k, u):
-        p = part(k, fbit[u % 2], u, 0)
+        p = part(k, fbit[u % 2], u, 1, True)
         return remote(p, p, k, 7 * U + u, first[u % 2])
 
     def c_ag(k, u):
@@ -330,32 +341,33 @@
         whole(rb)(k, u)
 
     hops = [
-        (c_rs, fold_core, f_rs),
-        (f_rs, fold(0, rf, ab, a_rs), a_rs),
-        (a_rs, fold(1, ra, sb, s_rs), s_rs),
-        (s_rs, whole(rs), b_rs),
-        (b_rs, last_fold, s_ag),
-        (s_ag, None, a_ag),
-        (a_ag, None, f_ag),
-        (f_ag, None, c_ag),
-        (c_ag, None, None),
+        ((c_rs,), fold_core, (f_rs,)),
+        ((f_rs,), fold(0, rf, ab, a_rs), (a_rs,)),
+        ((a_rs,), fold(1, ra, sb, s_rs), (s_rs,)),
+        ((s_rs,), whole(rs), (b_rs,)),
+        ((b_rs,), last_fold, (s_ag,)),
+        ((s_ag,), None, (a_ag, e_ag)),
+        ((a_ag,), None, (f_ag,)),
+        ((e_ag, f_ag), None, (c_ag,)),
+        ((c_ag,), None, ()),
     ]
 
     def serve(t, v, order):
         for h in order:
-            took, work, send = hops[h]
+            took, work, sent = hops[h]
             back = v - DELAY[h]
             k = t + back // U
             u = back % U
 
             @pl.when((k >= 0) & (k < nch))
             def _():
-                took(k, u).wait_recv()
+                for copy in took:
+                    copy(k, u).wait_recv()
                 if work is not None:
                     work(k, u)
-                if h >= 4 and send is not None:
-                    free(send, k, u)
-                if send is not None:
+                for send in sent:
+                    if h >= 4:
+                        free(send, k, u)
                     send(k, u).start()
 
     def grad_part(k, side):
@@ -494,7 +506,7 @@
             serve(t, v, ORDER)
         return carry
 
-    lax.fori_loop(nch + 2 * slots, nch + (DELAY[-1] + U - 1) // U + 1, late, 0)
+    lax.fori_loop(nch + 2 * slots, nch + (DELAY[-1] + U - 1) // U, late, 0)
     gb[...] = gb_v[5]
     for j in range(5):
         bias_hop(j).wait_send()
@@ -504,7 +516,7 @@
         back_send(j).wait_send()
     for k in range(nch - 2, nch):
         for u in range(U):
-            for f in (c_rs, f_rs, a_rs, s_rs, s_ag, a_ag, f_ag, c_ag):
+            for f in (c_rs, f_rs, a_rs, s_rs, s_ag, a_ag, e_ag, f_ag, c_ag):
                 f(k, u).wait_send()
 
 
@@ -569,7 +581,8 @@
             dma((7,)),
             dma((2,)),
             dma((2,)),
-            dma((2, 9 * U)),
+            dma((2, 10 * U)),
+            dma((4, U)),
             dma((4, U)),
             dma((2, 8 * U)),
             dma((5,)),

time: 115 us -> 115 us (level)
  no operation moved by 1% of the time
where the time goes in v6:
time: 115 us
  Pallas kernels  114 us (99%)
    pallas_call x1, Pallas kernels, main_call(): pl.pallas_call(main_kernel, out_shape=(pltpu.VMEM((total, width), bf16),...  104 us
    pallas_call x1, Pallas kernels, finish(): pl.pallas_call(finish_kernel, out_shape=(jax.ShapeDtypeStruct(act.shape,...  9.43 us

profile of v6, /device:TPU:0, one launch (start us, length us, event | category | flops | bytes accessed | tf_op | source)
XLA Modules:
  0.0 114.6 jit_solution(15580449559737667679)
XLA Ops:
  0.6 104.3 %layer.1 = (bf16[1408,2048]{1,0:T(8,128)(2,1)S(1)}, bf16[4,480,2048]{2,1,0:T(8,128)(2,1)S(1)}, bf16[16,2048,128]{2,1,0:T(8,128)(2,1)S(1)}, f32[1,2048]{1,0:T(1,128)S(1)}) custom-call(bf16[1408,2048]{1,0:T(8,128)(2,1)} %bitcast.9, bf16[2048,2048]{1,0:T(8,128)(2,1)} %w.1, f32[1,2048]{1,0:T(1,128)} %bitcast.15, bf16[1408,2048]{1,0:T(8,128)(2,1)} %bitcast.10, ...), custom_call_target="tpu_custom_call" | custom-call | tf_op jit(solution)/shard_map/layer/pallas_call | solution.py:540
  105.0 9.4 %finish.1 = (bf16[1408,2048]{1,0:T(8,128)(2,1)}, bf16[4,352,2048]{2,1,0:T(8,128)(2,1)}, f32[2048,2048]{1,0:T(8,128)}, f32[1,2048]{1,0:T(1,128)}) custom-call(bf16[1408,2048]{1,0:T(8,128)(2,1)S(1)} %get-tuple-element.12.act, bf16[4,480,2048]{2,1,0:T(8,128)(2,1)S(1)} %get-tuple-element.13.xr, bf16[16,2048,128]{2,1,0:T(8,128)(2,1)S(1)} %get-tuple-element.14.ag, ...), custom_call_target="tpu_custom_call" | custom-call | tf_op jit(solution)/shard_map/finish/pallas_call | solution.py:632

commit v7 on v6

--- a/solution.py
+++ b/solution.py
@@ -233,7 +233,7 @@
         return pltpu.make_async_remote_copy(
             src,
             dst,
-            ssem.at[k % 2, s],
+            ssem.at[s],
             rsem.at[k % 2, s - U],
             device_id=(to,),
             device_id_type=MESH,
@@ -258,7 +258,7 @@
         return pltpu.make_async_remote_copy(
             snd.at[k % 2, :, at(u, 0)],
             rc.at[k % 4, :, at(u, 0)],
-            ssem.at[k % 2, u],
+            ssem.at[u],
             rcsem.at[k % 4, u],
             device_id=(pc,),
             device_id_type=MESH,
@@ -289,7 +289,7 @@
         return pltpu.make_async_remote_copy(
             p,
             p,
-            ssem.at[k % 2, 9 * U + u],
+            ssem.at[9 * U + u],
             resem.at[k % 4, u],
             device_id=(first[u % 2],),
             device_id_type=MESH,
@@ -304,9 +304,9 @@
         return remote(p, p, k, 8 * U + u, pc)
 
     def free(send, k, u):
-        @pl.when(k >= 2)
+        @pl.when(k >= 1)
         def _():
-            send(k - 2, u).wait_send()
+            send(k - 1, u).wait_send()
 
     def fold_core(k, u):
         f = fbit[u % 2]
@@ -392,10 +392,10 @@
         serve(t, 0, ORDER)
         serve(t, 1, ORDER)
 
-        @pl.when(t >= 2)
+        @pl.when(t >= 1)
         def _():
             for u in range(U):
-                c_rs(t - 2, u).wait_send()
+                c_rs(t - 1, u).wait_send()
 
         if more:
             cot_in(t + 1).wait()
@@ -514,7 +514,7 @@
         for q in range(2):
             halo_send(j, q).wait_send()
         back_send(j).wait_send()
-    for k in range(nch - 2, nch):
+    for k in range(nch - 1, nch):
         for u in range(U):
             for f in (c_rs, f_rs, a_rs, s_rs, s_ag, a_ag, e_ag, f_ag, c_ag):
                 f(k, u).wait_send()
@@ -581,7 +581,7 @@
             dma((7,)),
             dma((2,)),
             dma((2,)),
-            dma((2, 10 * U)),
+            dma((10 * U,)),
             dma((4, U)),
             dma((4, U)),
             dma((2, 8 * U)),
@@ -640,9 +640,9 @@
         in_specs=[vmem] * 4,
         out_specs=[any_] * 4,
         scratch_shapes=[
-            pltpu.VMEM((4, 128, width), f32),
+            pltpu.VMEM((8, 64, width), f32),
             pltpu.SemaphoreType.DMA((2 + slots,)),
-            pltpu.SemaphoreType.DMA((4,)),
+            pltpu.SemaphoreType.DMA((8,)),
         ],
         compiler_params=pltpu.CompilerParams(vmem_limit_bytes=6 << 20),
         name="finish",

time: 115 us -> 114 us (level)
  no operation moved by 1% of the time
where the time goes in v7:
time: 114 us
  Pallas kernels  113 us (99%)
    pallas_call x1, Pallas kernels, main_call(): pl.pallas_call(main_kernel, out_shape=(pltpu.VMEM((total, width), bf16),...  104 us
    pallas_call x1, Pallas kernels, finish(): pl.pallas_call(finish_kernel, out_shape=(jax.ShapeDtypeStruct(act.shape,...  9.44 us

profile of v7, /device:TPU:0, one launch (start us, length us, event | category | flops | bytes accessed | tf_op | source)
XLA Modules:
  0.0 113.9 jit_solution(11599549368244217337)
XLA Ops:
  0.6 103.7 %layer.1 = (bf16[1408,2048]{1,0:T(8,128)(2,1)S(1)}, bf16[4,480,2048]{2,1,0:T(8,128)(2,1)S(1)}, bf16[16,2048,128]{2,1,0:T(8,128)(2,1)S(1)}, f32[1,2048]{1,0:T(1,128)S(1)}) custom-call(bf16[1408,2048]{1,0:T(8,128)(2,1)} %bitcast.9, bf16[2048,2048]{1,0:T(8,128)(2,1)} %w.1, f32[1,2048]{1,0:T(1,128)} %bitcast.15, bf16[1408,2048]{1,0:T(8,128)(2,1)} %bitcast.10, ...), custom_call_target="tpu_custom_call" | custom-call | tf_op jit(solution)/shard_map/layer/pallas_call | solution.py:540
  104.3 9.4 %finish.1 = (bf16[1408,2048]{1,0:T(8,128)(2,1)}, bf16[4,352,2048]{2,1,0:T(8,128)(2,1)}, f32[2048,2048]{1,0:T(8,128)}, f32[1,2048]{1,0:T(1,128)}) custom-call(bf16[1408,2048]{1,0:T(8,128)(2,1)S(1)} %get-tuple-element.12.act, bf16[4,480,2048]{2,1,0:T(8,128)(2,1)S(1)} %get-tuple-element.13.xr, bf16[16,2048,128]{2,1,0:T(8,128)(2,1)S(1)} %get-tuple-element.14.ag, ...), custom_call_target="tpu_custom_call" | custom-call | tf_op jit(solution)/shard_map/finish/pallas_call | solution.py:632
